TPU v7x, 512 devices: a whole 4x8x8 slice. The times are simulated.
512 devices in a mesh: gx: 32 (over y, x), gy: 16 (over z, core).
Axes of the slice: x: 4, y: 8, z: 8, core: 2. Of those that a mesh axis runs over, the one named last changes fastest.
Arguments:
- gradient: float32 [19, 64, 128, 128], P(None, 'gx', 'gy'), may hold values from -60 to 60
- steady_state: float32 [19, 64, 128, 128], P(None, 'gx', 'gy'), may hold values from 0.02 to 0.4
- enter_weight: float32 [128, 19], replicated, may hold values from -12 to 12
- middle_weight: float32 [128, 128], replicated, may hold values from -1.08 to 1.08
- leave_weight: float32 [19, 128], replicated, may hold values from -0.036 to 0.036
- links: int32 [2, 64, 128, 128], P(None, 'gx', 'gy'), may hold values from 0 to 1023, as said below
Outputs:
- adjoint: float32 [19, 64, 128, 128], P(None, 'gx', 'gy')
Inputs may be any that keep to these rules, and one draw needn't show every extreme that they name: Bit k of links is 1 exactly when the cell at offset c_k is solid or lies outside the lattice; about one cell in eight is solid, and one block of 3 x 3 x 3 cells is solid, so some cell has every bit set in both words.
All inputs are finite; a program needn't handle non-finite values.
Results may differ from a plain program's by a relative error of at most 0.0003.
Values sent between devices are 32-bit elements; how exact they have to be, the bound alone decides.
No kernel may reach another device: no remote copies, remote signals or barrier semaphores. Data moves between devices by JAX's collectives and lax.ppermute only.
A program may use at most 64 MiB of HBM per device.

v0:
```python
import jax
import jax.numpy as jnp
from jax import lax
from jax.experimental import pallas as pl
from jax.experimental.pallas import tpu as pltpu
from jax.sharding import PartitionSpec as P


Q = 19
HID = 128
ITERS = 3
ROWS = 24
SHRINK = 16.0
FLOOR = 1e-10
VMEM_BYTES = 16 * 1024 * 1024
SPAN = 6
FACE = 5

ORDER = (0, 4, 6, 8, 10, 2, 12, 14, 1, 5, 7, 9, 11, 3, 13, 15, 16, 17, 18)

F32 = jnp.float32
BF16 = jnp.bfloat16
VM = pl.BlockSpec(memory_space=pltpu.VMEM)
SM = pl.BlockSpec(memory_space=pltpu.SMEM)


def call(kernel, outs, *args):
    return pl.pallas_call(
        kernel,
        out_shape=[jax.ShapeDtypeStruct(shape, kind) for shape, kind in outs],
        in_specs=[SM if x.shape == (1,) else VM for x in args],
        out_specs=[VM] * len(outs),
        compiler_params=pltpu.CompilerParams(vmem_limit_bytes=VMEM_BYTES),
    )(*args)


def high(x):
    return x.astype(BF16).astype(F32)


def rows_dot(weights, x):
    top = high(x)
    stack = jnp.concatenate([top, top, x - top, jnp.zeros((8, x.shape[1]), F32)], axis=0)
    return jnp.dot(weights, stack.astype(BF16), preferred_element_type=F32)


def wide_dot(weights, x):
    top = x.astype(BF16)
    rest = (x - top.astype(F32)).astype(BF16)
    both = jnp.dot(weights, jnp.concatenate([top, rest], axis=0), preferred_element_type=F32)
    half = weights.shape[0] // 2
    return both[:half] + both[half:]


def together(chunks):
    chunks = list(chunks)
    for at in range(0, len(chunks), 4):
        running = chunks[at : at + 4]
        while running:
            running = [chunk for chunk in running if next(chunk, None)]


def weights_kernel(enter_t, middle, leave, enter_rows, leave_rows, middle_wide, middle_t_wide, enter_t_wide):
    def ordered(ref):
        rows = [ref[k : k + 1, :] for k in ORDER]
        return jnp.concatenate(rows + [jnp.zeros((ROWS - Q, HID), F32)], axis=0)

    def tall(rows):
        top = high(rows)
        stack = jnp.concatenate([top, rows - top, top, jnp.zeros((HID - 3 * ROWS, HID), F32)], axis=0)
        return stack.T.astype(BF16)

    def wide(mat):
        top = high(mat)
        rest = mat - top
        upper = jnp.concatenate([top, top], axis=1)
        lower = jnp.concatenate([rest, jnp.zeros_like(rest)], axis=1)
        return jnp.concatenate([upper, lower], axis=0).astype(BF16)

    enter = ordered(enter_t)
    enter_rows[...] = tall(enter)
    leave_rows[...] = tall(ordered(leave))
    middle_wide[...] = wide(middle[...])
    middle_t_wide[...] = wide(middle[...].T)
    scaled = enter * (1.0 / SHRINK)
    enter_t_wide[...] = wide(jnp.concatenate([scaled, jnp.zeros((8, HID), F32)], axis=0))


def offset_by(odd, low, high_):
    first = pl.multiple_of(jnp.where(odd, low, high_), 8)
    second = pl.multiple_of(jnp.where(odd, high_, low), 8)
    return first, second


def prepare_kernel(sx, sy, *refs):
    sources, (field, state, to_first, to_second), refs = refs[:3], refs[4:8], (refs[3], *refs[8:])
    odd, gradient, steady, links, sems = refs
    odd = odd[0] == 1
    copies = [
        pltpu.make_async_copy(source, target, sems.at[i])
        for i, (source, target) in enumerate(zip(sources, (gradient, steady, links)))
    ]
    for copy in copies:
        copy.start()
    blank = jnp.zeros((8, 128), F32)
    for x in range(sx):
        for y in range(sy):
            at = (x * sy + y) * ROWS + 16
            field[pl.ds(at, 8), :] = blank
            state[pl.ds(at, 8), :] = blank
    copies[0].wait()
    for x in range(sx):
        for row, k in enumerate(ORDER):
            field[pl.ds(x * sy * ROWS + row, sy, stride=ROWS), :] = gradient[k, x]
    copies[1].wait()
    copies[2].wait()
    for x in range(sx):
        for row, k in enumerate(ORDER):
            state[pl.ds(x * sy * ROWS + row, sy, stride=ROWS), :] = steady[k, x]
        for word in range(2):
            state[pl.ds(x * sy * ROWS + Q + word, sy, stride=ROWS), :] = links[word, x].astype(F32)
    at = 0
    for ref, depth in ((field, 3), (state, 2)):
        for x in range(sx):
            size = depth * ROWS
            first, second = offset_by(odd, x * sy * ROWS, (x * sy + sy - depth) * ROWS)
            to_first[pl.ds(at, size), :] = ref[pl.ds(first, size), :]
            to_second[pl.ds(at, size), :] = ref[pl.ds(second, size), :]
            at += size


def sublane():
    return lax.broadcasted_iota(jnp.int32, (8, 128), 0)


def row_constants(values):
    row = sublane()
    out = jnp.zeros((8, 128), jnp.int32)
    for at, value in enumerate(values):
        out = jnp.where(row == at, value, out)
    return out


def codes_of(tail):
    word_0 = jnp.broadcast_to(tail[3:4, :].astype(jnp.int32), (8, 128))
    word_1 = jnp.broadcast_to(tail[4:5, :].astype(jnp.int32), (8, 128))
    solid = (word_1 & (1 << (18 - 10))) != 0
    codes = []
    for group in range(3):
        members = [ORDER[group * 8 + i] if group * 8 + i < Q else -1 for i in range(8)]
        second = row_constants([1 if k >= 10 else 0 for k in members])
        bit = row_constants([0 if k < 0 else 1 << (k % 10) for k in members])
        pad = row_constants([1 if k < 0 else 0 for k in members])
        word = jnp.where(second == 1, word_1, word_0)
        code = jnp.where((word & bit) != 0, 1.0, 0.0)
        codes.append(jnp.where(jnp.logical_or(solid, pad == 1), 2.0, code))
    return codes


def slopes_of(columns, enter_rows, middle_wide, slope_one, slope_two, codes):
    enter = enter_rows[:, 0:80]
    middle = middle_wide[...]

    def chunk(at):
        pair = [ref[pl.ds(offset, ROWS), :] for ref, offset in columns[at : at + 2]]
        hidden = jnp.tanh(rows_dot(enter, jnp.concatenate(pair, axis=1)))
        yield True
        one = 1.0 - hidden * hidden
        hidden = jnp.tanh(wide_dot(middle, hidden))
        yield True
        two = 1.0 - hidden * hidden
        for i in range(2):
            slope_one[at + i] = one[:, i * 128 : (i + 1) * 128]
            slope_two[at + i] = two[:, i * 128 : (i + 1) * 128]
            for group, code in enumerate(codes_of(pair[i][16:24, :])):
                codes[at + i, group * 8 : group * 8 + 8, :] = code

    together(chunk(at) for at in range(0, len(columns), 2))


def own_slopes_kernel(count, state, enter_rows, middle_wide, slope_one, slope_two, codes):
    columns = [(state, i * ROWS) for i in range(count)]
    slopes_of(columns, enter_rows, middle_wide, slope_one, slope_two, codes)


def halo_slopes_kernel(sx, low, high_, enter_rows, middle_wide, slope_one, slope_two, codes):
    columns = []
    for x in range(sx):
        for ref in (low, high_):
            for row in range(2):
                columns.append((ref, (sx * 3 + x * 2 + row) * ROWS))
    slopes_of(columns, enter_rows, middle_wide, slope_one, slope_two, codes)


def face_shape(height, sz):
    return (-(-(height * FACE + 8 - FACE) // 8) * 8, sz)


def face(out, at, rows):
    out[pl.ds(at * FACE, FACE), :] = rows[0:FACE]


def face_tail(height, *outs):
    for out in outs:
        used = height * FACE
        out[pl.ds(used, out.shape[0] - used), :] = jnp.zeros((out.shape[0] - used, out.shape[1]), F32)


def faces_kernel(sx, sy, odd_x, odd_y, field, first, second, _, low, high_, to_first, to_second):
    odd = jnp.full((8, 128), odd_y[0]) == 1
    for at in range(0, first.shape[0], 8):
        one, two = first[pl.ds(at, 8), :], second[pl.ds(at, 8), :]
        low[pl.ds(at, 8), :] = jnp.where(odd, one, two)
        high_[pl.ds(at, 8), :] = jnp.where(odd, two, one)
    face_tail(sy + 6, to_first, to_second)
    odd = jnp.full((8, 128), odd_x[0]) == 1
    for row in range(-3, sy + 3):
        down = column(sy, field, low, high_, 0, row, 0)
        up = column(sy, field, low, high_, sx - 1, row, 8)
        face(to_first, row + 3, jnp.where(odd, down, up))
        face(to_second, row + 3, jnp.where(odd, up, down))


def column(sy, field, low, high_, x, row, group):
    if row < 0:
        return low[pl.ds((x * 3 + row + 3) * ROWS + group, 8), :]
    if row >= sy:
        return high_[pl.ds((x * 3 + row - sy) * ROWS + group, 8), :]
    return field[pl.ds((x * sy + row) * ROWS + group, 8), :]


def pull_column(get, code, x, row):
    at = sublane()
    straight = jnp.logical_or(at == 0, jnp.logical_or(at == 3, at == 4))
    first = jnp.logical_or(at == 3, at == 6)
    second = jnp.logical_or(at == 4, at == 7)
    own = [get(x, row, group) for group in (0, 8, 16)]
    out = []
    for group, step in ((0, 1), (8, -1)):
        value = jnp.where(straight, get(x + step, row, group), get(x, row + step, group))
        value = jnp.where(at == 1, get(x + step, row + step, group), value)
        value = jnp.where(at == 2, get(x + step, row - step, group), value)
        up = pltpu.roll(value, 127, 1)
        down = pltpu.roll(value, 1, 1)
        if step < 0:
            up, down = down, up
        out.append(jnp.where(first, up, jnp.where(second, down, value)))
    up = pltpu.roll(own[2], 127, 1)
    down = pltpu.roll(own[2], 1, 1)
    out.append(jnp.where(at == 0, up, jnp.where(at == 1, down, own[2])))
    swapped = jnp.where(at == 0, pltpu.roll(own[2], 7, 0), jnp.where(at == 1, pltpu.roll(own[2], 1, 0), own[2]))
    result = []
    for pulled, back, flag in zip(out, (own[1], own[0], swapped), (code(0), code(8), code(16))):
        result.append(jnp.where(flag == 0.0, pulled, jnp.where(flag == 1.0, back, 0.0)))
    return jnp.concatenate(result, axis=0)


def apply_rows(sx, first, last, get, table, leave_rows, middle_t_wide, enter_t_wide, put):
    leave = leave_rows[:, 0:80]
    middle = middle_t_wide[...]
    enter = enter_t_wide[...]

    def chunk(x, row):
        entries = [table(x, r) for r in range(row, min(row + SPAN, last))]
        reads = [
            pull_column(get, lambda g, codes=codes, at=at: codes[at, g : g + 8, :], x, row + i)
            for i, (_, _, codes, at) in enumerate(entries)
        ]
        read = jnp.concatenate(reads, axis=1)
        yield True
        carried = rows_dot(leave, read) * jnp.concatenate([two[at] for _, two, _, at in entries], axis=1)
        yield True
        carried = wide_dot(middle, carried) * jnp.concatenate([one[at] for one, _, _, at in entries], axis=1)
        yield True
        image = (0.5 / SHRINK) * read + wide_dot(enter, carried)[:ROWS]
        for i in range(len(entries)):
            put(x, row + i, image[:, i * 128 : (i + 1) * 128])

    together(chunk(x, row) for x in range(sx) for row in range(first, last, SPAN))


def table_of(sy, refs):
    one, two, codes, one_h, two_h, codes_h = refs

    def table(x, row):
        if 0 <= row < sy:
            return one, two, codes, x * sy + row
        return one_h, two_h, codes_h, x * 4 + (row + 2 if row < 0 else row - sy + 2)

    return table


def apply_kernel(sx, sy, step, *refs):
    odd_x, *refs = refs
    odd = jnp.full((8, 128), odd_x[0]) == 1
    if step == 1:
        field, low, high_ = refs[:3]
        refs = refs[3:]

        def inner(x, row, group):
            return column(sy, field, low, high_, x, row, group)

    else:
        previous = refs[0]
        refs = refs[1:]
        depth = 4 - step
        height = sy + 2 * depth

        def inner(x, row, group):
            return previous[pl.ds((x * height + row + depth) * ROWS + group, 8), :]

    first, second = refs[:2]
    table = table_of(sy, refs[2:8])
    leave_rows, middle_t_wide, enter_t_wide = refs[8:11]
    refs = refs[11:]
    before = 4 - step
    seen = {}

    def beside(row):
        if row not in seen:
            one = first[pl.ds((row + before) * FACE, 8), :]
            two = second[pl.ds((row + before) * FACE, 8), :]
            seen[row] = jnp.where(odd, one, two), jnp.where(odd, two, one)
        return seen[row]

    def get(x, row, group):
        if x < 0:
            return beside(row)[0]
        if x >= sx:
            return beside(row)[1]
        return inner(x, row, group)

    after = 3 - step
    height_out = sy + 2 * after
    if step < 3:
        image, to_first, to_second = refs
        face_tail(height_out, to_first, to_second)

        def put(x, row, value):
            image[pl.ds((x * height_out + row + after) * ROWS, ROWS), :] = value

        apply_rows(sx, -after, sy + after, get, table, leave_rows, middle_t_wide, enter_t_wide, put)
        one, two = offset_by(odd_x[0] == 1, 0, (sx - 1) * height_out * ROWS + 8)
        for row in range(height_out):
            face(to_first, row, image[pl.ds(one + row * ROWS, 8), :])
            face(to_second, row, image[pl.ds(two + row * ROWS, 8), :])
        return

    field, image_one, out = refs
    totals = [jnp.zeros((8, 128), F32) for _ in range(10)]

    def put(x, row, value):
        for group in (0, 8, 16):
            parts = (
                field[pl.ds((x * sy + row) * ROWS + group, 8), :],
                image_one[pl.ds((x * (sy + 4) + row + 2) * ROWS + group, 8), :],
                inner(x, row, group),
                value[group : group + 8],
            )
            at = 0
            for i in range(4):
                for j in range(i, 4):
                    totals[at] = totals[at] + parts[i] * parts[j]
                    at += 1

    apply_rows(sx, 0, sy, get, table, leave_rows, middle_t_wide, enter_t_wide, put)
    sums = jnp.concatenate(
        [jnp.sum(total, axis=0, keepdims=True) for total in totals] + [jnp.zeros((6, 128), F32)], axis=0
    )
    sums = jnp.broadcast_to(jnp.sum(sums, axis=1, keepdims=True), (16, 128))
    place = lax.broadcasted_iota(jnp.int32, (16, 128), 0) == lax.broadcasted_iota(jnp.int32, (16, 128), 1)
    line = jnp.sum(jnp.where(place, sums, 0.0), axis=0, keepdims=True)
    for i in range(out.shape[0]):
        out[i] = line


def least_squares(hess, target):
    rows = [list(line) for line in hess]
    target = list(target)
    for col in range(ITERS):
        upper = rows[col][col]
        lower = rows[col + 1][col]
        radius = jnp.sqrt(upper * upper + lower * lower)
        cosine = upper / radius
        sine = lower / radius
        for other in range(col, ITERS):
            first_value = rows[col][other]
            second_value = rows[col + 1][other]
            rows[col][other] = cosine * first_value + sine * second_value
            rows[col + 1][other] = cosine * second_value - sine * first_value
        first_value = target[col]
        second_value = target[col + 1]
        target[col] = cosine * first_value + sine * second_value
        target[col + 1] = cosine * second_value - sine * first_value
    coeffs = [None] * ITERS
    for col in reversed(range(ITERS)):
        accum = target[col]
        for other in range(col + 1, ITERS):
            accum = accum - rows[col][other] * coeffs[other]
        coeffs[col] = accum / rows[col][col]
    return coeffs


def finish_kernel(sx, sy, parts, gradient, image_one, image_two, out):
    total = parts[0]
    for i in range(1, parts.shape[0]):
        total = total + parts[i]
    total = jnp.broadcast_to(total, (8, 128))
    lane = lax.broadcasted_iota(jnp.int32, (8, 128), 1)
    gram = [[None] * 4 for _ in range(4)]
    at = 0
    for i in range(4):
        for j in range(i, 4):
            one = jnp.sum(jnp.where(lane == at, total, 0.0), axis=1, keepdims=True)
            gram[i][j] = gram[j][i] = jnp.broadcast_to(one, (8, 128))
            at += 1
    size = [jnp.sqrt(gram[i][i]) for i in range(4)]
    inverse = [1.0 / value for value in size]
    cosines = [[gram[i][j] * inverse[i] * inverse[j] for j in range(4)] for i in range(4)]
    zero = jnp.zeros((8, 128), F32)
    one = zero + 1.0
    lower = [[zero] * 4 for _ in range(4)]
    for i in range(4):
        for j in range(i + 1):
            value = one if i == j else cosines[i][j]
            for k in range(j):
                value = value - lower[i][k] * lower[j][k]
            lower[i][j] = jnp.sqrt(jnp.maximum(value, FLOOR)) if i == j else value / lower[j][j]
    hess = [[zero] * ITERS for _ in range(ITERS + 1)]
    for j in range(ITERS):
        ratio = SHRINK * size[j + 1] * inverse[j]
        for i in range(j + 2):
            hess[i][j] = lower[j][i] - ratio * lower[j + 1][i]
    coeffs = least_squares(hess, [one, zero, zero, zero])
    scaled = [coeffs[j] * size[0] * inverse[j] for j in range(ITERS)]
    for x in range(sx):
        for row, k in enumerate(ORDER):
            second = image_one[pl.ds((x * (sy + 4) + 2) * ROWS + row, sy, stride=ROWS), :]
            third = image_two[pl.ds((x * (sy + 2) + 1) * ROWS + row, sy, stride=ROWS), :]
            out[k, x] = scaled[0] * gradient[k, x] + scaled[1] * second + scaled[2] * third


def exchange(axis, to_first, to_second):
    count = lax.axis_size(axis)
    near = [(i, i ^ 1) for i in range(count)]
    far = [(i, ((i + 1) ^ 1) - 1) for i in range(1, count - 1)]
    second = lax.ppermute(to_second, axis, far)
    first = lax.ppermute(to_first, axis, near)
    return first, second


def per_device(gradient, steady_state, enter_weight, middle_weight, leave_weight, links):
    sx, sy, sz = gradient.shape[1:]
    own = sx * sy
    odd_x, odd_y = [(lax.axis_index(axis) % 2).reshape(1) for axis in ("gx", "gy")]

    def bind(kernel, *static):
        def bound(*refs):
            kernel(*static, *refs)

        bound.__name__ = kernel.__name__
        return bound

    flat = (own * ROWS, sz)
    message = (sx * 5 * ROWS, sz)
    field, state, to_first, to_second = pl.pallas_call(
        bind(prepare_kernel, sx, sy),
        out_shape=[jax.ShapeDtypeStruct(shape, F32) for shape in (flat, flat, message, message)],
        in_specs=[pl.BlockSpec(memory_space=pltpu.HBM)] * 3 + [SM],
        out_specs=[VM] * 4,
        scratch_shapes=[pltpu.VMEM(x.shape, x.dtype) for x in (gradient, steady_state, links)]
        + [pltpu.SemaphoreType.DMA((3,))],
        compiler_params=pltpu.CompilerParams(vmem_limit_bytes=VMEM_BYTES),
    )(*[pltpu.with_memory_space_constraint(x, pltpu.HBM) for x in (gradient, steady_state, links)], odd_y)
    first, second = exchange("gy", to_first, to_second)
    enter_rows, leave_rows, middle_wide, middle_t_wide, enter_t_wide = call(
        weights_kernel,
        [((HID, HID), BF16), ((HID, HID), BF16), ((2 * HID, 2 * HID), BF16), ((2 * HID, 2 * HID), BF16), ((64, 2 * HID), BF16)],
        enter_weight.T, middle_weight, leave_weight,
    )

    def tables(count):
        return [((count, HID, sz), F32), ((count, HID, sz), F32), ((count, ROWS, sz), F32)]

    own_table = call(bind(own_slopes_kernel, own), tables(own), state, enter_rows, middle_wide)
    low, high_, to_first, to_second = call(
        bind(faces_kernel, sx, sy),
        [(message, F32)] * 2 + [(face_shape(sy + 6, sz), F32)] * 2,
        odd_x, odd_y, field, first, second, own_table[2],
    )
    first, second = exchange("gx", to_first, to_second)
    halo_table = call(
        bind(halo_slopes_kernel, sx), tables(sx * 4), low, high_, enter_rows, middle_wide
    )
    shared = (*own_table, *halo_table, leave_rows, middle_t_wide, enter_t_wide)

    def image_shapes(depth):
        height = sy + 2 * depth
        return [((sx * height * ROWS, sz), F32), (face_shape(height, sz), F32), (face_shape(height, sz), F32)]

    image_one, to_first, to_second = call(
        bind(apply_kernel, sx, sy, 1), image_shapes(2), odd_x, field, low, high_, first, second, *shared
    )
    first, second = exchange("gx", to_first, to_second)
    image_two, to_first, to_second = call(
        bind(apply_kernel, sx, sy, 2), image_shapes(1), odd_x, image_one, first, second, *shared
    )
    first, second = exchange("gx", to_first, to_second)
    count_y = lax.axis_size("gy")
    count_x = lax.axis_size("gx")

    def last_kernel(*refs):
        *refs, field, image_one, out = refs
        apply_kernel(sx, sy, 3, *refs, field, image_one, out)

    (line,) = call(
        last_kernel, [((count_y, 1, sz), F32)], odd_x, image_two, first, second, *shared, field, image_one
    )
    line = jnp.sum(lax.all_to_all(line, "gy", 0, 0), axis=0, keepdims=True)
    parts = lax.all_to_all(jnp.broadcast_to(line, (count_x, 1, sz)), "gx", 0, 0)
    (adjoint,) = call(
        bind(finish_kernel, sx, sy), [(gradient.shape, F32)], parts, gradient, image_one, image_two
    )
    return adjoint


def solution(mesh):
    in_specs = (
        P(None, "gx", "gy", None),
        P(None, "gx", "gy", None),
        P(),
        P(),
        P(),
        P(None, "gx", "gy", None),
    )
    out_specs = P(None, "gx", "gy", None)
    return jax.shard_map(
        per_device, mesh=mesh, in_specs=in_specs, out_specs=out_specs, check_vma=False
    )
```

profile of v0, /device:TPU:1, one launch (start us, length us, event | category | flops | bytes accessed | tf_op | source)
XLA Modules:
  0.0 83.7 jit_solution(6977173385498783877)
XLA Ops:
  0.0 1.1 %shard_map.64 = (f32[384,128]{1,0:T(8,128)S(1)}, f32[384,128]{1,0:T(8,128)S(1)}, f32[240,128]{1,0:T(8,128)S(1)}, f32[240,128]{1,0:T(8,128)S(1)}) custom-call(f32[19,2,8,128]{3,2,1,0:T(8,128)} %refs_1_.3, f32[19,2,8,128]{3,2,1,0:T(8,128)} %refs_1_.2, s32[2,2,8,128]{3,2,1,0:T(8,128)} %refs_2_.1, s32[1]{0:T(128)} %bitcast.1.refs_3_.refs_1_), custom_call_target="tpu_custom_call" | custom-call | tf_op jit(solution)/shard_map/pallas_call | solution.py:466
  1.1 8.7 %collective-permute-start = (f32[240,128]{1,0:T(8,128)S(1)}, f32[240,128]{1,0:T(8,128)S(1)}, u32[]{:S(2)}, u32[]{:S(2)}) collective-permute-start(f32[240,128]{1,0:T(8,128)S(1)} %get-tuple-element.31), channel_id=1, source_target_pairs={{0,1},{1,0},{2,3},{3,2},{4,5},{5,4},{6,7},{7,6},{8,9},{9,8},{10,11... | collective-permute-start | bytes 368648 | tf_op jit(solution)/shard_map/ppermute | solution.py:448
  9.9 1.9 %collective-permute-start.1 = (f32[240,128]{1,0:T(8,128)S(1)}, f32[240,128]{1,0:T(8,128)S(1)}, u32[]{:S(2)}, u32[]{:S(2)}) collective-permute-start(f32[240,128]{1,0:T(8,128)S(1)} %get-tuple-element.32), channel_id=1, source_target_pairs={{1,2},{2,1},{3,4},{4,3},{5,6},{6,5},{7,8},{8,7},{9,10},{10,9},{11,... | collective-permute-start | bytes 368648 | tf_op jit(solution)/shard_map/ppermute | solution.py:447
  11.8 0.7 copy-done.2
  12.5 0.0 copy-done.3
  12.5 0.1 shard_map.65
  12.6 0.8 %shard_map.66 = (f32[16,128,128]{2,1,0:T(8,128)S(1)}, f32[16,128,128]{2,1,0:T(8,128)S(1)}, f32[16,24,128]{2,1,0:T(8,128)S(1)}) custom-call(f32[384,128]{1,0:T(8,128)S(1)} %get-tuple-element.33.refs_0_, bf16[128,128]{1,0:T(8,128)(2,1)S(1)} %get-tuple-element.34.refs_1_.refs_2_, bf16[256,256]{1,0:T(8,128)(2,1)S(1)} %get-tuple-element.35.refs_2_.refs_3_), custom_call_target="tpu_custom_call" | custom-call | tf_op jit(solution)/shard_map/pallas_call | solution.py:28
  13.5 2.6 %collective-permute-done.1.refs_4_ = f32[240,128]{1,0:T(8,128)S(1)} collective-permute-done((f32[240,128]{1,0:T(8,128)S(1)}, f32[240,128]{1,0:T(8,128)S(1)}, u32[]{:S(2)}, u32[]{:S(2)}) %collective-permute-start.1) | collective-permute-done | bytes 122912 | tf_op jit(solution)/shard_map/ppermute | solution.py:447
  16.1 1.9 %collective-permute-start.2 = (f32[80,128]{1,0:T(8,128)S(1)}, f32[80,128]{1,0:T(8,128)S(1)}, u32[]{:S(2)}, u32[]{:S(2)}) collective-permute-start(f32[80,128]{1,0:T(8,128)S(1)} %get-tuple-element.39), channel_id=1, source_target_pairs={{0,16},{16,0},{32,48},{48,32},{64,80},{80,64},{96,112},{112,96},{1... | collective-permute-start | bytes 122888 | tf_op jit(solution)/shard_map/ppermute | solution.py:448
  18.0 0.7 collective-permute-start.3
  18.7 0.5 shard_map.68
  19.2 1.6 %collective-permute-done.2.refs_4_ = f32[80,128]{1,0:T(8,128)S(1)} collective-permute-done((f32[80,128]{1,0:T(8,128)S(1)}, f32[80,128]{1,0:T(8,128)S(1)}, u32[]{:S(2)}, u32[]{:S(2)}) %collective-permute-start.2) | collective-permute-done | bytes 40992 | tf_op jit(solution)/shard_map/ppermute | solution.py:448
  20.8 1.2 %shard_map.69 = (f32[576,128]{1,0:T(8,128)S(1)}, f32[64,128]{1,0:T(8,128)S(1)}, f32[64,128]{1,0:T(8,128)S(1)}) custom-call(s32[1]{0:T(128)} %bitcast.refs_0_, f32[384,128]{1,0:T(8,128)S(1)} %get-tuple-element.30.refs_2_.refs_1_.refs_13_, f32[240,128]{1,0:T(8,128)S(1)} %get-tuple-element.37.refs_0_.refs_2_, f32[240,128]{1,0:T(8,128)S(1)} %get-tuple-element.38.refs_1_.refs_3_, ...), custom_call_target="tpu_custom_call" | custom-call | tf_op jit(solution)/shard_map/pallas_call | solution.py:28
  22.1 5.3 %collective-permute-start.4 = (f32[64,128]{1,0:T(8,128)S(1)}, f32[64,128]{1,0:T(8,128)S(1)}, u32[]{:S(2)}, u32[]{:S(2)}) collective-permute-start(f32[64,128]{1,0:T(8,128)S(1)} %get-tuple-element.50), channel_id=1, source_target_pairs={{0,16},{16,0},{32,48},{48,32},{64,80},{80,64},{96,112},{112,96},{1... | collective-permute-start | bytes 98312 | tf_op jit(solution)/shard_map/ppermute | solution.py:448
  27.4 0.7 collective-permute-start.5
  28.1 0.6 collective-permute-done.4.refs_2_
  28.7 1.0 %shard_map.70 = (f32[480,128]{1,0:T(8,128)S(1)}, f32[56,128]{1,0:T(8,128)S(1)}, f32[56,128]{1,0:T(8,128)S(1)}) custom-call(s32[1]{0:T(128)} %bitcast.refs_0_, f32[576,128]{1,0:T(8,128)S(1)} %get-tuple-element.49.refs_1_.refs_14_.refs_2_, f32[64,128]{1,0:T(8,128)S(1)} %collective-permute-done.4.refs_2_, f32[64,128]{1,0:T(8,128)S(1)} %collective-permute-done.5.refs_3_, ...), custom_call_target="tpu_custom_call" | custom-call | tf_op jit(solution)/shard_map/pallas_call | solution.py:28
  29.7 5.3 %collective-permute-start.6 = (f32[56,128]{1,0:T(8,128)S(1)}, f32[56,128]{1,0:T(8,128)S(1)}, u32[]{:S(2)}, u32[]{:S(2)}) collective-permute-start(f32[56,128]{1,0:T(8,128)S(1)} %get-tuple-element.53), channel_id=1, source_target_pairs={{0,16},{16,0},{32,48},{48,32},{64,80},{80,64},{96,112},{112,96},{1... | collective-permute-start | bytes 86024 | tf_op jit(solution)/shard_map/ppermute | solution.py:448
  35.0 0.7 collective-permute-start.7
  35.7 0.6 collective-permute-done.6.refs_2_
  36.3 1.0 %shard_map.71 = f32[16,1,128]{2,1,0:T(1,128)S(1)} custom-call(s32[1]{0:T(128)} %bitcast.refs_0_, f32[480,128]{1,0:T(8,128)S(1)} %get-tuple-element.52.refs_1_.refs_3_, f32[56,128]{1,0:T(8,128)S(1)} %collective-permute-done.6.refs_2_, f32[56,128]{1,0:T(8,128)S(1)} %collective-permute-done.7.refs_3_, f32[16,128,128]{2,1,0:T(8,128)S(1)} %get-tuple-element.41.refs_6_.refs_4_, ...), custom_call_target="tpu_custom_call" | custom-call | tf_op jit(solution)/shard_map/pallas_call | solution.py:28
  37.3 19.5 %all_to_all.10 = f32[16,1,128]{2,1,0:T(1,128)S(1)} all-to-all(f32[16,1,128]{2,1,0:T(1,128)S(1)} %shard_map.71), channel_id=1, replica_groups=mesh['gx'=32,'gy'=16] {'gy'}, dimensions={0} | all-to-all | bytes 16384 | tf_op jit(solution)/shard_map/all_to_all | solution.py:519
  56.8 25.9 %all_to_all.11.refs_0_ = f32[32,1,128]{2,1,0:T(1,128)S(1)} all-to-all(f32[32,1,128]{2,1,0:T(1,128)S(1)} %broadcast_in_dim.2), channel_id=1, replica_groups=mesh['gx'=32,'gy'=16] {'gx'}, dimensions={0} | all-to-all | bytes 32768 | tf_op jit(solution)/shard_map/all_to_all | solution.py:520
  82.8 0.9 %shard_map.72 = f32[19,2,8,128]{3,2,1,0:T(8,128)} custom-call(f32[32,1,128]{2,1,0:T(1,128)S(1)} %all_to_all.11.refs_0_, f32[19,2,8,128]{3,2,1,0:T(8,128)S(1)} %copy-done, f32[576,128]{1,0:T(8,128)S(1)} %get-tuple-element.49.refs_1_.refs_14_.refs_2_, f32[480,128]{1,0:T(8,128)S(1)} %get-tuple-element.52.refs_1_.refs_3_), custom_call_target="tpu_custom_call" | custom-call | tf_op jit(solution)/shard_map/pallas_call | solution.py:28
  (13 shorter events, 0.1 us)
Async XLA Ops:
  0.0 11.8 %copy-start.1 = (f32[128,128]{1,0:T(8,128)S(1)}, f32[128,128]{1,0:T(8,128)}, u32[]{:S(2)}) copy-start(f32[128,128]{1,0:T(8,128)} %middle.1) | copy-start | bytes 196612
  1.1 12.4 %collective-permute-start = (f32[240,128]{1,0:T(8,128)S(1)}, f32[240,128]{1,0:T(8,128)S(1)}, u32[]{:S(2)}, u32[]{:S(2)}) collective-permute-start(f32[240,128]{1,0:T(8,128)S(1)} %get-tuple-element.31), channel_id=1, source_target_pairs={{0,1},{1,0},{2,3},{3,2},{4,5},{5,4},{6,7},{7,6},{8,9},{9,8},{10,11... | collective-permute-start | bytes 368648 | tf_op jit(solution)/shard_map/ppermute | solution.py:448
  9.9 6.2 %collective-permute-start.1 = (f32[240,128]{1,0:T(8,128)S(1)}, f32[240,128]{1,0:T(8,128)S(1)}, u32[]{:S(2)}, u32[]{:S(2)}) collective-permute-start(f32[240,128]{1,0:T(8,128)S(1)} %get-tuple-element.32), channel_id=1, source_target_pairs={{1,2},{2,1},{3,4},{4,3},{5,6},{6,5},{7,8},{8,7},{9,10},{10,9},{11,... | collective-permute-start | bytes 368648 | tf_op jit(solution)/shard_map/ppermute | solution.py:447
  11.8 0.7 copy-start.2
  11.8 0.7 copy-start.3
  16.1 4.7 %collective-permute-start.2 = (f32[80,128]{1,0:T(8,128)S(1)}, f32[80,128]{1,0:T(8,128)S(1)}, u32[]{:S(2)}, u32[]{:S(2)}) collective-permute-start(f32[80,128]{1,0:T(8,128)S(1)} %get-tuple-element.39), channel_id=1, source_target_pairs={{0,16},{16,0},{32,48},{48,32},{64,80},{80,64},{96,112},{112,96},{1... | collective-permute-start | bytes 122888 | tf_op jit(solution)/shard_map/ppermute | solution.py:448
  18.0 2.8 %collective-permute-start.3 = (f32[80,128]{1,0:T(8,128)S(1)}, f32[80,128]{1,0:T(8,128)S(1)}, u32[]{:S(2)}, u32[]{:S(2)}) collective-permute-start(f32[80,128]{1,0:T(8,128)S(1)} %get-tuple-element.40), channel_id=1, source_target_pairs={{16,32},{32,16},{48,64},{64,48},{80,96},{96,80},{112,128},{128,112... | collective-permute-start | bytes 122888 | tf_op jit(solution)/shard_map/ppermute | solution.py:447
  22.1 6.6 %collective-permute-start.4 = (f32[64,128]{1,0:T(8,128)S(1)}, f32[64,128]{1,0:T(8,128)S(1)}, u32[]{:S(2)}, u32[]{:S(2)}) collective-permute-start(f32[64,128]{1,0:T(8,128)S(1)} %get-tuple-element.50), channel_id=1, source_target_pairs={{0,16},{16,0},{32,48},{48,32},{64,80},{80,64},{96,112},{112,96},{1... | collective-permute-start | bytes 98312 | tf_op jit(solution)/shard_map/ppermute | solution.py:448
  27.4 1.3 %collective-permute-start.5 = (f32[64,128]{1,0:T(8,128)S(1)}, f32[64,128]{1,0:T(8,128)S(1)}, u32[]{:S(2)}, u32[]{:S(2)}) collective-permute-start(f32[64,128]{1,0:T(8,128)S(1)} %get-tuple-element.51), channel_id=1, source_target_pairs={{16,32},{32,16},{48,64},{64,48},{80,96},{96,80},{112,128},{128,112... | collective-permute-start | bytes 98312 | tf_op jit(solution)/shard_map/ppermute | solution.py:447
  29.7 6.5 %collective-permute-start.6 = (f32[56,128]{1,0:T(8,128)S(1)}, f32[56,128]{1,0:T(8,128)S(1)}, u32[]{:S(2)}, u32[]{:S(2)}) collective-permute-start(f32[56,128]{1,0:T(8,128)S(1)} %get-tuple-element.53), channel_id=1, source_target_pairs={{0,16},{16,0},{32,48},{48,32},{64,80},{80,64},{96,112},{112,96},{1... | collective-permute-start | bytes 86024 | tf_op jit(solution)/shard_map/ppermute | solution.py:448
  35.0 1.2 %collective-permute-start.7 = (f32[56,128]{1,0:T(8,128)S(1)}, f32[56,128]{1,0:T(8,128)S(1)}, u32[]{:S(2)}, u32[]{:S(2)}) collective-permute-start(f32[56,128]{1,0:T(8,128)S(1)} %get-tuple-element.54), channel_id=1, source_target_pairs={{16,32},{32,16},{48,64},{64,48},{80,96},{96,80},{112,128},{128,112... | collective-permute-start | bytes 86024 | tf_op jit(solution)/shard_map/ppermute | solution.py:447
  36.3 46.5 %copy-start = (f32[19,2,8,128]{3,2,1,0:T(8,128)S(1)}, f32[19,2,8,128]{3,2,1,0:T(8,128)}, u32[]{:S(2)}) copy-start(f32[19,2,8,128]{3,2,1,0:T(8,128)} %refs_1_.3) | copy-start | bytes 466948
where the time goes:
time: 84.3 us; the launch traced here: 83.7 us
  blocking collectives  45.4 us (54%)
  starting transfers between devices  25.2 us (30%)
  Pallas kernels  6.8 us (8%)
  waiting for transfers between devices  5.38 us (6%)
    all_to_all x1, blocking collectives, per_device(): parts = lax.all_to_all(jnp.broadcast_to(line, (count_x, 1, sz)), 'gx', 0, 0)  25.9 us
    ppermute x4, starting transfers between devices, exchange(): first = lax.ppermute(to_first, axis, near)  21.2 us
    all_to_all x1, blocking collectives, per_device(): line = jnp.sum(lax.all_to_all(line, 'gy', 0, 0), axis=0, keepdims=True)  19.5 us
    pallas_call x8, Pallas kernels, call(): pl.pallas_call(kernel, out_shape=[jax.ShapeDtypeStruct(shape, kind) for s...  5.71 us
    ppermute x4, starting transfers between devices, exchange(): second = lax.ppermute(to_second, axis, far)  3.91 us
    ppermute x4, waiting for transfers between devices, exchange(): first = lax.ppermute(to_first, axis, near)  2.82 us
    ppermute x4, waiting for transfers between devices, exchange(): second = lax.ppermute(to_second, axis, far)  2.56 us
  transfers between devices with their start and end apart: 8, of which 4 were waited for; matrix products, arithmetic and copies ran while one was open for 0% of the time, Pallas kernels for 2%

commit v1 on v0

--- a/solution.py
+++ b/solution.py
@@ -93,12 +93,12 @@
 
 
 def prepare_kernel(sx, sy, *refs):
-    sources, (field, state, to_first, to_second), refs = refs[:3], refs[4:8], (refs[3], *refs[8:])
-    odd, gradient, steady, links, sems = refs
+    sources, odd, (field, state, to_first, to_second) = refs[:6], refs[6], refs[7:11]
+    weights, (gradient, steady, links, sems) = refs[11:14], refs[14:]
     odd = odd[0] == 1
     copies = [
         pltpu.make_async_copy(source, target, sems.at[i])
-        for i, (source, target) in enumerate(zip(sources, (gradient, steady, links)))
+        for i, (source, target) in enumerate(zip(sources, (gradient, steady, links, *weights)))
     ]
     for copy in copies:
         copy.start()
@@ -127,6 +127,8 @@
             to_first[pl.ds(at, size), :] = ref[pl.ds(first, size), :]
             to_second[pl.ds(at, size), :] = ref[pl.ds(second, size), :]
             at += size
+    for copy in copies[3:]:
+        copy.wait()
 
 
 def sublane():
@@ -463,20 +465,22 @@
 
     flat = (own * ROWS, sz)
     message = (sx * 5 * ROWS, sz)
-    field, state, to_first, to_second = pl.pallas_call(
+    fetched = (gradient, steady_state, links, enter_weight.T, middle_weight, leave_weight)
+    field, state, to_first, to_second, *fetched_weights = pl.pallas_call(
         bind(prepare_kernel, sx, sy),
-        out_shape=[jax.ShapeDtypeStruct(shape, F32) for shape in (flat, flat, message, message)],
-        in_specs=[pl.BlockSpec(memory_space=pltpu.HBM)] * 3 + [SM],
-        out_specs=[VM] * 4,
+        out_shape=[jax.ShapeDtypeStruct(shape, F32) for shape in (flat, flat, message, message)]
+        + [jax.ShapeDtypeStruct(x.shape, x.dtype) for x in fetched[3:]],
+        in_specs=[pl.BlockSpec(memory_space=pltpu.HBM)] * 6 + [SM],
+        out_specs=[VM] * 7,
         scratch_shapes=[pltpu.VMEM(x.shape, x.dtype) for x in (gradient, steady_state, links)]
-        + [pltpu.SemaphoreType.DMA((3,))],
+        + [pltpu.SemaphoreType.DMA((6,))],
         compiler_params=pltpu.CompilerParams(vmem_limit_bytes=VMEM_BYTES),
-    )(*[pltpu.with_memory_space_constraint(x, pltpu.HBM) for x in (gradient, steady_state, links)], odd_y)
+    )(*[pltpu.with_memory_space_constraint(x, pltpu.HBM) for x in fetched], odd_y)
     first, second = exchange("gy", to_first, to_second)
     enter_rows, leave_rows, middle_wide, middle_t_wide, enter_t_wide = call(
         weights_kernel,
         [((HID, HID), BF16), ((HID, HID), BF16), ((2 * HID, 2 * HID), BF16), ((2 * HID, 2 * HID), BF16), ((64, 2 * HID), BF16)],
-        enter_weight.T, middle_weight, leave_weight,
+        *fetched_weights,
     )
 
     def tables(count):

time: 84.3 us -> 84.1 us (level)
  no operation moved by 1% of the time
where the time goes in v1:
time: 84.1 us; the launch traced here: 83.7 us
  blocking collectives  45.5 us (54%)
  starting transfers between devices  25.2 us (30%)
  Pallas kernels  6.81 us (8%)
  waiting for transfers between devices  6.1 us (7%)
    all_to_all x1, blocking collectives, per_device(): parts = lax.all_to_all(jnp.broadcast_to(line, (count_x, 1, sz)), 'gx', 0, 0)  25.9 us
    ppermute x4, starting transfers between devices, exchange(): first = lax.ppermute(to_first, axis, near)  21.2 us
    all_to_all x1, blocking collectives, per_device(): line = jnp.sum(lax.all_to_all(line, 'gy', 0, 0), axis=0, keepdims=True)  19.5 us
    pallas_call x8, Pallas kernels, call(): pl.pallas_call(kernel, out_shape=[jax.ShapeDtypeStruct(shape, kind) for s...  5.72 us
    ppermute x4, starting transfers between devices, exchange(): second = lax.ppermute(to_second, axis, far)  3.91 us
    ppermute x4, waiting for transfers between devices, exchange(): second = lax.ppermute(to_second, axis, far)  3.28 us
    ppermute x4, waiting for transfers between devices, exchange(): first = lax.ppermute(to_first, axis, near)  2.82 us
  transfers between devices with their start and end apart: 8, of which 4 were waited for; matrix products, arithmetic and copies ran while one was open for 0% of the time, Pallas kernels for 2%

profile of v1, /device:TPU:1, one launch (start us, length us, event | category | flops | bytes accessed | tf_op | source)
XLA Modules:
  0.0 83.7 jit_solution(8039114634914813851)
XLA Ops:
  0.0 1.1 %shard_map.64 = (f32[384,128]{1,0:T(8,128)S(1)}, f32[384,128]{1,0:T(8,128)S(1)}, f32[240,128]{1,0:T(8,128)S(1)}, f32[240,128]{1,0:T(8,128)S(1)}, f32[19,128]{1,0...) custom-call(f32[19,2,8,128]{3,2,1,0:T(8,128)} %refs_1_.3, f32[19,2,8,128]{3,2,1,0:T(8,128)} %refs_1_.2, ...), custom_call_target="tpu_custom_call" | custom-call | tf_op jit(solution)/shard_map/pallas_call | solution.py:469
  1.1 8.7 %collective-permute-start = (f32[240,128]{1,0:T(8,128)S(1)}, f32[240,128]{1,0:T(8,128)S(1)}, u32[]{:S(2)}, u32[]{:S(2)}) collective-permute-start(f32[240,128]{1,0:T(8,128)S(1)} %get-tuple-element.34), channel_id=1, source_target_pairs={{0,1},{1,0},{2,3},{3,2},{4,5},{5,4},{6,7},{7,6},{8,9},{9,8},{10,11... | collective-permute-start | bytes 368648 | tf_op jit(solution)/shard_map/ppermute | solution.py:450
  9.9 1.9 %collective-permute-start.1 = (f32[240,128]{1,0:T(8,128)S(1)}, f32[240,128]{1,0:T(8,128)S(1)}, u32[]{:S(2)}, u32[]{:S(2)}) collective-permute-start(f32[240,128]{1,0:T(8,128)S(1)} %get-tuple-element.35), channel_id=1, source_target_pairs={{1,2},{2,1},{3,4},{4,3},{5,6},{6,5},{7,8},{8,7},{9,10},{10,9},{11,... | collective-permute-start | bytes 368648 | tf_op jit(solution)/shard_map/ppermute | solution.py:449
  11.8 0.1 shard_map.65
  11.9 0.8 %shard_map.66 = (f32[16,128,128]{2,1,0:T(8,128)S(1)}, f32[16,128,128]{2,1,0:T(8,128)S(1)}, f32[16,24,128]{2,1,0:T(8,128)S(1)}) custom-call(f32[384,128]{1,0:T(8,128)S(1)} %get-tuple-element.36.refs_0_, bf16[128,128]{1,0:T(8,128)(2,1)S(1)} %get-tuple-element.40.refs_1_.refs_2_, bf16[256,256]{1,0:T(8,128)(2,1)S(1)} %get-tuple-element.41.refs_2_.refs_3_), custom_call_target="tpu_custom_call" | custom-call | tf_op jit(solution)/shard_map/pallas_call | solution.py:28
  12.8 0.0 collective-permute-done.refs_3_
  12.8 3.3 %collective-permute-done.1.refs_4_ = f32[240,128]{1,0:T(8,128)S(1)} collective-permute-done((f32[240,128]{1,0:T(8,128)S(1)}, f32[240,128]{1,0:T(8,128)S(1)}, u32[]{:S(2)}, u32[]{:S(2)}) %collective-permute-start.1) | collective-permute-done | bytes 122912 | tf_op jit(solution)/shard_map/ppermute | solution.py:449
  16.1 1.9 %collective-permute-start.2 = (f32[80,128]{1,0:T(8,128)S(1)}, f32[80,128]{1,0:T(8,128)S(1)}, u32[]{:S(2)}, u32[]{:S(2)}) collective-permute-start(f32[80,128]{1,0:T(8,128)S(1)} %get-tuple-element.45), channel_id=1, source_target_pairs={{0,16},{16,0},{32,48},{48,32},{64,80},{80,64},{96,112},{112,96},{1... | collective-permute-start | bytes 122888 | tf_op jit(solution)/shard_map/ppermute | solution.py:450
  18.0 0.7 collective-permute-start.3
  18.7 0.5 shard_map.68
  19.2 1.6 %collective-permute-done.2.refs_4_ = f32[80,128]{1,0:T(8,128)S(1)} collective-permute-done((f32[80,128]{1,0:T(8,128)S(1)}, f32[80,128]{1,0:T(8,128)S(1)}, u32[]{:S(2)}, u32[]{:S(2)}) %collective-permute-start.2) | collective-permute-done | bytes 40992 | tf_op jit(solution)/shard_map/ppermute | solution.py:450
  20.8 1.2 %shard_map.69 = (f32[576,128]{1,0:T(8,128)S(1)}, f32[64,128]{1,0:T(8,128)S(1)}, f32[64,128]{1,0:T(8,128)S(1)}) custom-call(s32[1]{0:T(128)} %bitcast.refs_0_, f32[384,128]{1,0:T(8,128)S(1)} %get-tuple-element.33.refs_2_.refs_1_.refs_13_, f32[240,128]{1,0:T(8,128)S(1)} %get-tuple-element.43.refs_0_.refs_2_, f32[240,128]{1,0:T(8,128)S(1)} %get-tuple-element.44.refs_1_.refs_3_, ...), custom_call_target="tpu_custom_call" | custom-call | tf_op jit(solution)/shard_map/pallas_call | solution.py:28
  22.1 5.3 %collective-permute-start.4 = (f32[64,128]{1,0:T(8,128)S(1)}, f32[64,128]{1,0:T(8,128)S(1)}, u32[]{:S(2)}, u32[]{:S(2)}) collective-permute-start(f32[64,128]{1,0:T(8,128)S(1)} %get-tuple-element.56), channel_id=1, source_target_pairs={{0,16},{16,0},{32,48},{48,32},{64,80},{80,64},{96,112},{112,96},{1... | collective-permute-start | bytes 98312 | tf_op jit(solution)/shard_map/ppermute | solution.py:450
  27.4 0.7 collective-permute-start.5
  28.1 0.6 collective-permute-done.4.refs_2_
  28.7 0.0 collective-permute-done.5.refs_3_
  28.7 1.0 %shard_map.70 = (f32[480,128]{1,0:T(8,128)S(1)}, f32[56,128]{1,0:T(8,128)S(1)}, f32[56,128]{1,0:T(8,128)S(1)}) custom-call(s32[1]{0:T(128)} %bitcast.refs_0_, f32[576,128]{1,0:T(8,128)S(1)} %get-tuple-element.55.refs_1_.refs_14_.refs_2_, f32[64,128]{1,0:T(8,128)S(1)} %collective-permute-done.4.refs_2_, f32[64,128]{1,0:T(8,128)S(1)} %collective-permute-done.5.refs_3_, ...), custom_call_target="tpu_custom_call" | custom-call | tf_op jit(solution)/shard_map/pallas_call | solution.py:28
  29.7 5.3 %collective-permute-start.6 = (f32[56,128]{1,0:T(8,128)S(1)}, f32[56,128]{1,0:T(8,128)S(1)}, u32[]{:S(2)}, u32[]{:S(2)}) collective-permute-start(f32[56,128]{1,0:T(8,128)S(1)} %get-tuple-element.59), channel_id=1, source_target_pairs={{0,16},{16,0},{32,48},{48,32},{64,80},{80,64},{96,112},{112,96},{1... | collective-permute-start | bytes 86024 | tf_op jit(solution)/shard_map/ppermute | solution.py:450
  35.0 0.7 collective-permute-start.7
  35.7 0.6 collective-permute-done.6.refs_2_
  36.3 1.0 %shard_map.71 = f32[16,1,128]{2,1,0:T(1,128)S(1)} custom-call(s32[1]{0:T(128)} %bitcast.refs_0_, f32[480,128]{1,0:T(8,128)S(1)} %get-tuple-element.58.refs_1_.refs_3_, f32[56,128]{1,0:T(8,128)S(1)} %collective-permute-done.6.refs_2_, f32[56,128]{1,0:T(8,128)S(1)} %collective-permute-done.7.refs_3_, f32[16,128,128]{2,1,0:T(8,128)S(1)} %get-tuple-element.47.refs_6_.refs_4_, ...), custom_call_target="tpu_custom_call" | custom-call | tf_op jit(solution)/shard_map/pallas_call | solution.py:28
  37.3 19.5 %all_to_all.10 = f32[16,1,128]{2,1,0:T(1,128)S(1)} all-to-all(f32[16,1,128]{2,1,0:T(1,128)S(1)} %shard_map.71), channel_id=1, replica_groups=mesh['gx'=32,'gy'=16] {'gy'}, dimensions={0} | all-to-all | bytes 16384 | tf_op jit(solution)/shard_map/all_to_all | solution.py:523
  56.8 25.9 %all_to_all.11.refs_0_ = f32[32,1,128]{2,1,0:T(1,128)S(1)} all-to-all(f32[32,1,128]{2,1,0:T(1,128)S(1)} %broadcast_in_dim.2), channel_id=1, replica_groups=mesh['gx'=32,'gy'=16] {'gx'}, dimensions={0} | all-to-all | bytes 32768 | tf_op jit(solution)/shard_map/all_to_all | solution.py:524
  82.8 0.9 %shard_map.72 = f32[19,2,8,128]{3,2,1,0:T(8,128)} custom-call(f32[32,1,128]{2,1,0:T(1,128)S(1)} %all_to_all.11.refs_0_, f32[19,2,8,128]{3,2,1,0:T(8,128)S(1)} %copy-done, f32[576,128]{1,0:T(8,128)S(1)} %get-tuple-element.55.refs_1_.refs_14_.refs_2_, f32[480,128]{1,0:T(8,128)S(1)} %get-tuple-element.58.refs_1_.refs_3_), custom_call_target="tpu_custom_call" | custom-call | tf_op jit(solution)/shard_map/pallas_call | solution.py:28
  (7 shorter events, 0.1 us)
Async XLA Ops:
  1.1 11.7 %collective-permute-start = (f32[240,128]{1,0:T(8,128)S(1)}, f32[240,128]{1,0:T(8,128)S(1)}, u32[]{:S(2)}, u32[]{:S(2)}) collective-permute-start(f32[240,128]{1,0:T(8,128)S(1)} %get-tuple-element.34), channel_id=1, source_target_pairs={{0,1},{1,0},{2,3},{3,2},{4,5},{5,4},{6,7},{7,6},{8,9},{9,8},{10,11... | collective-permute-start | bytes 368648 | tf_op jit(solution)/shard_map/ppermute | solution.py:450
  9.9 6.2 %collective-permute-start.1 = (f32[240,128]{1,0:T(8,128)S(1)}, f32[240,128]{1,0:T(8,128)S(1)}, u32[]{:S(2)}, u32[]{:S(2)}) collective-permute-start(f32[240,128]{1,0:T(8,128)S(1)} %get-tuple-element.35), channel_id=1, source_target_pairs={{1,2},{2,1},{3,4},{4,3},{5,6},{6,5},{7,8},{8,7},{9,10},{10,9},{11,... | collective-permute-start | bytes 368648 | tf_op jit(solution)/shard_map/ppermute | solution.py:449
  16.1 4.7 %collective-permute-start.2 = (f32[80,128]{1,0:T(8,128)S(1)}, f32[80,128]{1,0:T(8,128)S(1)}, u32[]{:S(2)}, u32[]{:S(2)}) collective-permute-start(f32[80,128]{1,0:T(8,128)S(1)} %get-tuple-element.45), channel_id=1, source_target_pairs={{0,16},{16,0},{32,48},{48,32},{64,80},{80,64},{96,112},{112,96},{1... | collective-permute-start | bytes 122888 | tf_op jit(solution)/shard_map/ppermute | solution.py:450
  18.0 2.8 %collective-permute-start.3 = (f32[80,128]{1,0:T(8,128)S(1)}, f32[80,128]{1,0:T(8,128)S(1)}, u32[]{:S(2)}, u32[]{:S(2)}) collective-permute-start(f32[80,128]{1,0:T(8,128)S(1)} %get-tuple-element.46), channel_id=1, source_target_pairs={{16,32},{32,16},{48,64},{64,48},{80,96},{96,80},{112,128},{128,112... | collective-permute-start | bytes 122888 | tf_op jit(solution)/shard_map/ppermute | solution.py:449
  22.1 6.6 %collective-permute-start.4 = (f32[64,128]{1,0:T(8,128)S(1)}, f32[64,128]{1,0:T(8,128)S(1)}, u32[]{:S(2)}, u32[]{:S(2)}) collective-permute-start(f32[64,128]{1,0:T(8,128)S(1)} %get-tuple-element.56), channel_id=1, source_target_pairs={{0,16},{16,0},{32,48},{48,32},{64,80},{80,64},{96,112},{112,96},{1... | collective-permute-start | bytes 98312 | tf_op jit(solution)/shard_map/ppermute | solution.py:450
  27.4 1.3 %collective-permute-start.5 = (f32[64,128]{1,0:T(8,128)S(1)}, f32[64,128]{1,0:T(8,128)S(1)}, u32[]{:S(2)}, u32[]{:S(2)}) collective-permute-start(f32[64,128]{1,0:T(8,128)S(1)} %get-tuple-element.57), channel_id=1, source_target_pairs={{16,32},{32,16},{48,64},{64,48},{80,96},{96,80},{112,128},{128,112... | collective-permute-start | bytes 98312 | tf_op jit(solution)/shard_map/ppermute | solution.py:449
  29.7 6.5 %collective-permute-start.6 = (f32[56,128]{1,0:T(8,128)S(1)}, f32[56,128]{1,0:T(8,128)S(1)}, u32[]{:S(2)}, u32[]{:S(2)}) collective-permute-start(f32[56,128]{1,0:T(8,128)S(1)} %get-tuple-element.59), channel_id=1, source_target_pairs={{0,16},{16,0},{32,48},{48,32},{64,80},{80,64},{96,112},{112,96},{1... | collective-permute-start | bytes 86024 | tf_op jit(solution)/shard_map/ppermute | solution.py:450
  35.0 1.2 %collective-permute-start.7 = (f32[56,128]{1,0:T(8,128)S(1)}, f32[56,128]{1,0:T(8,128)S(1)}, u32[]{:S(2)}, u32[]{:S(2)}) collective-permute-start(f32[56,128]{1,0:T(8,128)S(1)} %get-tuple-element.60), channel_id=1, source_target_pairs={{16,32},{32,16},{48,64},{64,48},{80,96},{96,80},{112,128},{128,112... | collective-permute-start | bytes 86024 | tf_op jit(solution)/shard_map/ppermute | solution.py:449
  36.3 46.5 %copy-start = (f32[19,2,8,128]{3,2,1,0:T(8,128)S(1)}, f32[19,2,8,128]{3,2,1,0:T(8,128)}, u32[]{:S(2)}) copy-start(f32[19,2,8,128]{3,2,1,0:T(8,128)} %refs_1_.3) | copy-start | bytes 466948

commit v2 on v1

--- a/solution.py
+++ b/solution.py
@@ -13,7 +13,7 @@
 SHRINK = 16.0
 FLOOR = 1e-10
 VMEM_BYTES = 16 * 1024 * 1024
-SPAN = 6
+SPANS = (6, 6, 6)
 FACE = 5
 
 ORDER = (0, 4, 6, 8, 10, 2, 12, 14, 1, 5, 7, 9, 11, 3, 13, 15, 16, 17, 18)
@@ -164,7 +164,7 @@
     middle = middle_wide[...]
 
     def chunk(at):
-        pair = [ref[pl.ds(offset, ROWS), :] for ref, offset in columns[at : at + 2]]
+        pair = [load() for load in columns[at : at + 2]]
         hidden = jnp.tanh(rows_dot(enter, jnp.concatenate(pair, axis=1)))
         yield True
         one = 1.0 - hidden * hidden
@@ -180,8 +180,12 @@
     together(chunk(at) for at in range(0, len(columns), 2))
 
 
+def loader(ref, offset):
+    return lambda: ref[pl.ds(offset, ROWS), :]
+
+
 def own_slopes_kernel(count, state, enter_rows, middle_wide, slope_one, slope_two, codes):
-    columns = [(state, i * ROWS) for i in range(count)]
+    columns = [loader(state, i * ROWS) for i in range(count)]
     slopes_of(columns, enter_rows, middle_wide, slope_one, slope_two, codes)
 
 
@@ -190,37 +194,64 @@
     for x in range(sx):
         for ref in (low, high_):
             for row in range(2):
-                columns.append((ref, (sx * 3 + x * 2 + row) * ROWS))
+                columns.append(loader(ref, (sx * 3 + x * 2 + row) * ROWS))
     slopes_of(columns, enter_rows, middle_wide, slope_one, slope_two, codes)
 
 
-def face_shape(height, sz):
-    return (-(-(height * FACE + 8 - FACE) // 8) * 8, sz)
-
-
-def face(out, at, rows):
-    out[pl.ds(at * FACE, FACE), :] = rows[0:FACE]
-
-
-def face_tail(height, *outs):
+def side_slopes_kernel(sy, odd_x, first, second, enter_rows, middle_wide, slope_one, slope_two, codes):
+    odd = jnp.full((ROWS, 128), odd_x[0]) == 1
+    base = face_rows(sy + 6)
+
+    def side(one, two, row):
+        at = pl.ds(base + row * ROWS, ROWS)
+        return lambda: jnp.where(odd, one[at, :], two[at, :])
+
+    columns = [side(first, second, row) for row in range(sy + 2)]
+    columns += [side(second, first, row) for row in range(sy + 2)]
+    slopes_of(columns, enter_rows, middle_wide, slope_one, slope_two, codes)
+
+
+def face_rows(height):
+    return -(-(height * FACE + 8 - FACE) // 8) * 8
+
+
+def face(out, base, at, rows):
+    out[pl.ds(base + at * FACE, FACE), :] = rows[0:FACE]
+
+
+def face_tail(base, height, *outs):
+    used, size = height * FACE, face_rows(height)
     for out in outs:
-        used = height * FACE
-        out[pl.ds(used, out.shape[0] - used), :] = jnp.zeros((out.shape[0] - used, out.shape[1]), F32)
-
-
-def faces_kernel(sx, sy, odd_x, odd_y, field, first, second, _, low, high_, to_first, to_second):
+        out[pl.ds(base + used, size - used), :] = jnp.zeros((size - used, out.shape[1]), F32)
+
+
+def faces_kernel(sx, sy, odd_x, odd_y, field, state, first, second, _, low, high_, to_first, to_second):
     odd = jnp.full((8, 128), odd_y[0]) == 1
     for at in range(0, first.shape[0], 8):
         one, two = first[pl.ds(at, 8), :], second[pl.ds(at, 8), :]
         low[pl.ds(at, 8), :] = jnp.where(odd, one, two)
         high_[pl.ds(at, 8), :] = jnp.where(odd, two, one)
-    face_tail(sy + 6, to_first, to_second)
+    face_tail(0, sy + 6, to_first, to_second)
     odd = jnp.full((8, 128), odd_x[0]) == 1
     for row in range(-3, sy + 3):
         down = column(sy, field, low, high_, 0, row, 0)
         up = column(sy, field, low, high_, sx - 1, row, 8)
-        face(to_first, row + 3, jnp.where(odd, down, up))
-        face(to_second, row + 3, jnp.where(odd, up, down))
+        face(to_first, 0, row + 3, jnp.where(odd, down, up))
+        face(to_second, 0, row + 3, jnp.where(odd, up, down))
+
+    def state_column(x, row, group):
+        if row < 0:
+            return low[pl.ds((sx * 3 + x * 2 + row + 2) * ROWS + group, 8), :]
+        if row >= sy:
+            return high_[pl.ds((sx * 3 + x * 2 + row - sy) * ROWS + group, 8), :]
+        return state[pl.ds((x * sy + row) * ROWS + group, 8), :]
+
+    for row in range(-1, sy + 1):
+        for group in (0, 8, 16):
+            down, up = state_column(0, row, group), state_column(sx - 1, row, group)
+            at = face_rows(sy + 6) + (row + 1) * ROWS + group
+            to_first[pl.ds(at, 8), :] = jnp.where(odd, down, up)
+            to_second[pl.ds(at, 8), :] = jnp.where(odd, up, down)
 
 
 def column(sy, field, low, high_, x, row, group):
@@ -257,13 +288,11 @@
     return jnp.concatenate(result, axis=0)
 
 
-def apply_rows(sx, first, last, get, table, leave_rows, middle_t_wide, enter_t_wide, put):
-    leave = leave_rows[:, 0:80]
-    middle = middle_t_wide[...]
-    enter = enter_t_wide[...]
+def apply_rows(xs, first, last, get, table, weights, put, span):
+    leave, middle, enter = weights[0][:, 0:80], weights[1][...], weights[2][...]
 
     def chunk(x, row):
-        entries = [table(x, r) for r in range(row, min(row + SPAN, last))]
+        entries = [table(x, r) for r in range(row, min(row + span, last))]
         reads = [
             pull_column(get, lambda g, codes=codes, at=at: codes[at, g : g + 8, :], x, row + i)
             for i, (_, _, codes, at) in enumerate(entries)
@@ -278,13 +307,15 @@
         for i in range(len(entries)):
             put(x, row + i, image[:, i * 128 : (i + 1) * 128])
 
-    together(chunk(x, row) for x in range(sx) for row in range(first, last, SPAN))
-
-
-def table_of(sy, refs):
+    together(chunk(x, row) for x in xs for row in range(first, last, span))
+
+
+def table_of(sx, sy, refs, side=None):
     one, two, codes, one_h, two_h, codes_h = refs
 
     def table(x, row):
+        if not 0 <= x < sx:
+            return *side, (row + 1 if x < 0 else sy + 2 + row + 1)
         if 0 <= row < sy:
             return one, two, codes, x * sy + row
         return one_h, two_h, codes_h, x * 4 + (row + 2 if row < 0 else row - sy + 2)
@@ -292,63 +323,69 @@
     return table
 
 
-def apply_kernel(sx, sy, step, *refs):
-    odd_x, *refs = refs
-    odd = jnp.full((8, 128), odd_x[0]) == 1
-    if step == 1:
-        field, low, high_ = refs[:3]
-        refs = refs[3:]
-
-        def inner(x, row, group):
-            return column(sy, field, low, high_, x, row, group)
-
-    else:
-        previous = refs[0]
-        refs = refs[1:]
-        depth = 4 - step
-        height = sy + 2 * depth
-
-        def inner(x, row, group):
-            return previous[pl.ds((x * height + row + depth) * ROWS + group, 8), :]
-
-    first, second = refs[:2]
-    table = table_of(sy, refs[2:8])
-    leave_rows, middle_t_wide, enter_t_wide = refs[8:11]
-    refs = refs[11:]
-    before = 4 - step
+def sorted_loads(odd, first, second):
     seen = {}
 
-    def beside(row):
-        if row not in seen:
-            one = first[pl.ds((row + before) * FACE, 8), :]
-            two = second[pl.ds((row + before) * FACE, 8), :]
-            seen[row] = jnp.where(odd, one, two), jnp.where(odd, two, one)
-        return seen[row]
+    def get(at):
+        if at not in seen:
+            one, two = first[pl.ds(at, 8), :], second[pl.ds(at, 8), :]
+            seen[at] = jnp.where(odd, one, two), jnp.where(odd, two, one)
+        return seen[at]
+
+    return get
+
+
+def first_kernel(sx, sy, odd_x, field, low, high_, first, second, *refs):
+    tables, weights, (image, to_first, to_second) = refs[:6], refs[6:9], refs[9:]
+    beside = sorted_loads(jnp.full((8, 128), odd_x[0]) == 1, first, second)
+    height = sy + 4
 
     def get(x, row, group):
         if x < 0:
-            return beside(row)[0]
+            return beside((row + 3) * FACE)[0]
         if x >= sx:
-            return beside(row)[1]
-        return inner(x, row, group)
-
-    after = 3 - step
-    height_out = sy + 2 * after
-    if step < 3:
-        image, to_first, to_second = refs
-        face_tail(height_out, to_first, to_second)
-
-        def put(x, row, value):
-            image[pl.ds((x * height_out + row + after) * ROWS, ROWS), :] = value
-
-        apply_rows(sx, -after, sy + after, get, table, leave_rows, middle_t_wide, enter_t_wide, put)
-        one, two = offset_by(odd_x[0] == 1, 0, (sx - 1) * height_out * ROWS + 8)
-        for row in range(height_out):
-            face(to_first, row, image[pl.ds(one + row * ROWS, 8), :])
-            face(to_second, row, image[pl.ds(two + row * ROWS, 8), :])
-        return
-
-    field, image_one, out = refs
+            return beside((row + 3) * FACE)[1]
+        return column(sy, field, low, high_, x, row, group)
+
+    def put(x, row, value):
+        image[pl.ds((x * height + row + 2) * ROWS, ROWS), :] = value
+
+    near = height * ROWS
+    face_tail(near, height, to_first, to_second)
+    apply_rows(range(sx), -2, sy + 2, get, table_of(sx, sy, tables), weights, put, SPANS[0])
+    odd = odd_x[0] == 1
+    columns = offset_by(odd, 0, (sx - 1) * near)
+    faces = offset_by(odd, near, (sx - 2) * near + 8)
+    for out, at, face_at in zip((to_first, to_second), columns, faces):
+        out[pl.ds(0, near), :] = image[pl.ds(at, near), :]
+        for row in range(height):
+            face(out, near, row, image[pl.ds(face_at + row * ROWS, 8), :])
+
+
+def second_kernel(sx, sy, odd_x, previous, first, second, *refs):
+    tables, side, weights, image = refs[:6], refs[6:9], refs[9:12], refs[12]
+    beside = sorted_loads(jnp.full((8, 128), odd_x[0]) == 1, first, second)
+    height = sy + 4
+
+    def get(x, row, group):
+        if 0 <= x < sx:
+            return previous[pl.ds((x * height + row + 2) * ROWS + group, 8), :]
+        if x in (-1, sx):
+            return beside((row + 2) * ROWS + group)[0 if x < 0 else 1]
+        return beside(height * ROWS + (row + 2) * FACE)[0 if x < 0 else 1]
+
+    def put(x, row, value):
+        image[pl.ds(((x + 1) * (sy + 2) + row + 1) * ROWS, ROWS), :] = value
+
+    apply_rows(range(-1, sx + 1), -1, sy + 1, get, table_of(sx, sy, tables, side), weights, put, SPANS[1])
+
+
+def third_kernel(sx, sy, previous, *refs):
+    tables, weights, (field, image_one, out) = refs[:6], refs[6:9], refs[9:]
+
+    def get(x, row, group):
+        return previous[pl.ds(((x + 1) * (sy + 2) + row + 1) * ROWS + group, 8), :]
+
     totals = [jnp.zeros((8, 128), F32) for _ in range(10)]
 
     def put(x, row, value):
@@ -356,7 +393,7 @@
             parts = (
                 field[pl.ds((x * sy + row) * ROWS + group, 8), :],
                 image_one[pl.ds((x * (sy + 4) + row + 2) * ROWS + group, 8), :],
-                inner(x, row, group),
+                get(x, row, group),
                 value[group : group + 8],
             )
             at = 0
@@ -365,7 +402,7 @@
                     totals[at] = totals[at] + parts[i] * parts[j]
                     at += 1
 
-    apply_rows(sx, 0, sy, get, table, leave_rows, middle_t_wide, enter_t_wide, put)
+    apply_rows(range(sx), 0, sy, get, table_of(sx, sy, tables), weights, put, SPANS[2])
     sums = jnp.concatenate(
         [jnp.sum(total, axis=0, keepdims=True) for total in totals] + [jnp.zeros((6, 128), F32)], axis=0
     )
@@ -438,7 +475,7 @@
     for x in range(sx):
         for row, k in enumerate(ORDER):
             second = image_one[pl.ds((x * (sy + 4) + 2) * ROWS + row, sy, stride=ROWS), :]
-            third = image_two[pl.ds((x * (sy + 2) + 1) * ROWS + row, sy, stride=ROWS), :]
+            third = image_two[pl.ds(((x + 1) * (sy + 2) + 1) * ROWS + row, sy, stride=ROWS), :]
             out[k, x] = scaled[0] * gradient[k, x] + scaled[1] * second + scaled[2] * third
 
 
@@ -489,36 +526,37 @@
     own_table = call(bind(own_slopes_kernel, own), tables(own), state, enter_rows, middle_wide)
     low, high_, to_first, to_second = call(
         bind(faces_kernel, sx, sy),
-        [(message, F32)] * 2 + [(face_shape(sy + 6, sz), F32)] * 2,
-        odd_x, odd_y, field, first, second, own_table[2],
+        [(message, F32)] * 2 + [((face_rows(sy + 6) + (sy + 2) * ROWS, sz), F32)] * 2,
+        odd_x, odd_y, field, state, first, second, own_table[2],
     )
     first, second = exchange("gx", to_first, to_second)
     halo_table = call(
         bind(halo_slopes_kernel, sx), tables(sx * 4), low, high_, enter_rows, middle_wide
     )
-    shared = (*own_table, *halo_table, leave_rows, middle_t_wide, enter_t_wide)
-
-    def image_shapes(depth):
-        height = sy + 2 * depth
-        return [((sx * height * ROWS, sz), F32), (face_shape(height, sz), F32), (face_shape(height, sz), F32)]
-
+    tables_here, weights = (*own_table, *halo_table), (leave_rows, middle_t_wide, enter_t_wide)
+    height = sy + 4
+    side_message = (height * ROWS + face_rows(height), sz)
     image_one, to_first, to_second = call(
-        bind(apply_kernel, sx, sy, 1), image_shapes(2), odd_x, field, low, high_, first, second, *shared
+        bind(first_kernel, sx, sy),
+        [((sx * height * ROWS, sz), F32), (side_message, F32), (side_message, F32)],
+        odd_x, field, low, high_, first, second, *tables_here, *weights,
+    )
+    side_table = call(
+        bind(side_slopes_kernel, sy), tables(2 * (sy + 2)), odd_x, first, second, enter_rows, middle_wide
     )
     first, second = exchange("gx", to_first, to_second)
-    image_two, to_first, to_second = call(
-        bind(apply_kernel, sx, sy, 2), image_shapes(1), odd_x, image_one, first, second, *shared
-    )
-    first, second = exchange("gx", to_first, to_second)
+    (image_two,) = call(
+        bind(second_kernel, sx, sy),
+        [(((sx + 2) * (sy + 2) * ROWS, sz), F32)],
+        odd_x, image_one, first, second, *tables_here, *side_table, *weights,
+    )
     count_y = lax.axis_size("gy")
     count_x = lax.axis_size("gx")
 
-    def last_kernel(*refs):
-        *refs, field, image_one, out = refs
-        apply_kernel(sx, sy, 3, *refs, field, image_one, out)
-
     (line,) = call(
-        last_kernel, [((count_y, 1, sz), F32)], odd_x, image_two, first, second, *shared, field, image_one
+        bind(third_kernel, sx, sy),
+        [((count_y, 1, sz), F32)],
+        image_two, *tables_here, *weights, field, image_one,
     )
     line = jnp.sum(lax.all_to_all(line, "gy", 0, 0), axis=0, keepdims=True)
     parts = lax.all_to_all(jnp.broadcast_to(line, (count_x, 1, sz)), "gx", 0, 0)

time: 84.1 us -> 77 us (0.916)
  starting transfers between devices: 25.2 us -> 19.2 us
  blocking collectives: 45.5 us -> 41.1 us
  Pallas kernels: 6.81 us -> 8.84 us
  waiting for transfers between devices: 6.1 us -> 7.28 us
    ppermute x4 -> x3, starting transfers between devices: 21.2 us -> 16 us  [exchange(): first = lax.ppermute(to_first, axis, near)]
    all_to_all x1, blocking collectives: 19.5 us -> 16.4 us  [per_device(): line = jnp.sum(lax.all_to_all(line, 'gy', 0, 0), axis=0, keepdims=True)]
    pallas_call x8 -> x9, Pallas kernels: 5.72 us -> 7.75 us  [call(): pl.pallas_call(kernel, out_shape=[jax.ShapeDtypeStruct(shape, kind) for s...]
    all_to_all x1, blocking collectives: 25.9 us -> 24.7 us  [per_device(): parts = lax.all_to_all(jnp.broadcast_to(line, (count_x, 1, sz)), 'gx', 0, 0)]
    ppermute x4 -> x3, waiting for transfers between devices: 2.82 us -> 4.01 us  [exchange(): first = lax.ppermute(to_first, axis, near)]
    ppermute x4 -> x3, starting transfers between devices: 3.91 us -> 3.26 us  [exchange(): second = lax.ppermute(to_second, axis, far)]
    ppermute x4 -> x3, waiting for transfers between devices: 3.28 us -> 3.27 us  [exchange(): second = lax.ppermute(to_second, axis, far)]
  transfers between devices with their start and end apart: 8 -> 6, of which waited for: 4 -> 3; matrix products, arithmetic and copies ran while one was open for 0% -> 0% of each run, Pallas kernels for 2% -> 3%
where the time goes in v2:
time: 77 us; the launch traced here: 76.7 us
  blocking collectives  41.1 us (53%)
  starting transfers between devices  19.2 us (25%)
  Pallas kernels  8.84 us (11%)
  waiting for transfers between devices  7.28 us (9%)
    all_to_all x1, blocking collectives, per_device(): parts = lax.all_to_all(jnp.broadcast_to(line, (count_x, 1, sz)), 'gx', 0, 0)  24.7 us
    all_to_all x1, blocking collectives, per_device(): line = jnp.sum(lax.all_to_all(line, 'gy', 0, 0), axis=0, keepdims=True)  16.4 us
    ppermute x3, starting transfers between devices, exchange(): first = lax.ppermute(to_first, axis, near)  16 us
    pallas_call x9, Pallas kernels, call(): pl.pallas_call(kernel, out_shape=[jax.ShapeDtypeStruct(shape, kind) for s...  7.75 us
    ppermute x3, waiting for transfers between devices, exchange(): first = lax.ppermute(to_first, axis, near)  4.01 us
    ppermute x3, waiting for transfers between devices, exchange(): second = lax.ppermute(to_second, axis, far)  3.27 us
    ppermute x3, starting transfers between devices, exchange(): second = lax.ppermute(to_second, axis, far)  3.26 us
  transfers between devices with their start and end apart: 6, of which 3 were waited for; matrix products, arithmetic and copies ran while one was open for 0% of the time, Pallas kernels for 3%

profile of v2, /device:TPU:1, one launch (start us, length us, event | category | flops | bytes accessed | tf_op | source)
XLA Modules:
  0.0 76.7 jit_solution(4925458214937286064)
XLA Ops:
  0.0 1.1 %shard_map.64 = (f32[384,128]{1,0:T(8,128)S(1)}, f32[384,128]{1,0:T(8,128)S(1)}, f32[240,128]{1,0:T(8,128)S(1)}, f32[240,128]{1,0:T(8,128)S(1)}, f32[19,128]{1,0...) custom-call(f32[19,2,8,128]{3,2,1,0:T(8,128)} %refs_1_.3, f32[19,2,8,128]{3,2,1,0:T(8,128)} %refs_1_.2, ...), custom_call_target="tpu_custom_call" | custom-call | tf_op jit(solution)/shard_map/pallas_call | solution.py:506
  1.1 8.7 %collective-permute-start = (f32[240,128]{1,0:T(8,128)S(1)}, f32[240,128]{1,0:T(8,128)S(1)}, u32[]{:S(2)}, u32[]{:S(2)}) collective-permute-start(f32[240,128]{1,0:T(8,128)S(1)} %get-tuple-element.35), channel_id=1, source_target_pairs={{0,1},{1,0},{2,3},{3,2},{4,5},{5,4},{6,7},{7,6},{8,9},{9,8},{10,11... | collective-permute-start | bytes 368648 | tf_op jit(solution)/shard_map/ppermute | solution.py:487
  9.9 1.9 %collective-permute-start.1 = (f32[240,128]{1,0:T(8,128)S(1)}, f32[240,128]{1,0:T(8,128)S(1)}, u32[]{:S(2)}, u32[]{:S(2)}) collective-permute-start(f32[240,128]{1,0:T(8,128)S(1)} %get-tuple-element.36), channel_id=1, source_target_pairs={{1,2},{2,1},{3,4},{4,3},{5,6},{6,5},{7,8},{8,7},{9,10},{10,9},{11,... | collective-permute-start | bytes 368648 | tf_op jit(solution)/shard_map/ppermute | solution.py:486
  11.8 0.1 shard_map.65
  11.9 0.8 %shard_map.66 = (f32[16,128,128]{2,1,0:T(8,128)S(1)}, f32[16,128,128]{2,1,0:T(8,128)S(1)}, f32[16,24,128]{2,1,0:T(8,128)S(1)}) custom-call(f32[384,128]{1,0:T(8,128)S(1)} %get-tuple-element.34.refs_0_.refs_3_, bf16[128,128]{1,0:T(8,128)(2,1)S(1)} %get-tuple-element.40.refs_1_.refs_2_.refs_3_, bf16[256,256]{1,0:T(8,128)(2,1)S(1)} %get-tuple-element.41.refs_2_.refs_3_.refs_4_), custom_call_target="tpu_custom_call" | custom-call | tf_op jit(solution)/shard_map/pallas_call | solution.py:28
  12.8 0.0 collective-permute-done.refs_4_
  12.8 3.3 %collective-permute-done.1.refs_5_ = f32[240,128]{1,0:T(8,128)S(1)} collective-permute-done((f32[240,128]{1,0:T(8,128)S(1)}, f32[240,128]{1,0:T(8,128)S(1)}, u32[]{:S(2)}, u32[]{:S(2)}) %collective-permute-start.1) | collective-permute-done | bytes 122912 | tf_op jit(solution)/shard_map/ppermute | solution.py:486
  16.1 1.9 %collective-permute-start.2 = (f32[320,128]{1,0:T(8,128)S(1)}, f32[320,128]{1,0:T(8,128)S(1)}, u32[]{:S(2)}, u32[]{:S(2)}) collective-permute-start(f32[320,128]{1,0:T(8,128)S(1)} %get-tuple-element.45), channel_id=1, source_target_pairs={{0,16},{16,0},{32,48},{48,32},{64,80},{80,64},{96,112},{112,96},{1... | collective-permute-start | bytes 491528 | tf_op jit(solution)/shard_map/ppermute | solution.py:487
  18.0 0.7 collective-permute-start.3
  18.7 0.5 shard_map.68
  19.2 2.9 %collective-permute-done.2.refs_4_.refs_1_ = f32[320,128]{1,0:T(8,128)S(1)} collective-permute-done((f32[320,128]{1,0:T(8,128)S(1)}, f32[320,128]{1,0:T(8,128)S(1)}, u32[]{:S(2)}, u32[]{:S(2)}) %collective-permute-start.2) | collective-permute-done | bytes 163872 | tf_op jit(solution)/shard_map/ppermute | solution.py:487
  22.2 0.0 collective-permute-done.3.refs_5_.refs_2_
  22.2 1.3 %shard_map.69 = (f32[576,128]{1,0:T(8,128)S(1)}, f32[352,128]{1,0:T(8,128)S(1)}, f32[352,128]{1,0:T(8,128)S(1)}) custom-call(s32[1]{0:T(128)} %bitcast.refs_0_, f32[384,128]{1,0:T(8,128)S(1)} %get-tuple-element.33.refs_2_.refs_1_.refs_10_, f32[240,128]{1,0:T(8,128)S(1)} %get-tuple-element.43.refs_0_.refs_2_, ...), custom_call_target="tpu_custom_call" | custom-call | tf_op jit(solution)/shard_map/pallas_call | solution.py:28
  23.5 5.3 %collective-permute-start.4 = (f32[352,128]{1,0:T(8,128)S(1)}, f32[352,128]{1,0:T(8,128)S(1)}, u32[]{:S(2)}, u32[]{:S(2)}) collective-permute-start(f32[352,128]{1,0:T(8,128)S(1)} %get-tuple-element.56), channel_id=1, source_target_pairs={{0,16},{16,0},{32,48},{48,32},{64,80},{80,64},{96,112},{112,96},{1... | collective-permute-start | bytes 540680 | tf_op jit(solution)/shard_map/ppermute | solution.py:487
  28.7 0.7 collective-permute-start.5
  29.4 1.1 %shard_map.70 = (f32[20,128,128]{2,1,0:T(8,128)S(1)}, f32[20,128,128]{2,1,0:T(8,128)S(1)}, f32[20,24,128]{2,1,0:T(8,128)S(1)}) custom-call(s32[1]{0:T(128)} %bitcast.refs_0_, f32[320,128]{1,0:T(8,128)S(1)} %collective-permute-done.2.refs_4_.refs_1_, f32[320,128]{1,0:T(8,128)S(1)} %collective-permute-done.3.refs_5_.refs_2_, ...), custom_call_target="tpu_custom_call" | custom-call | tf_op jit(solution)/shard_map/pallas_call | solution.py:28
  30.5 1.1 %collective-permute-done.4.refs_2_ = f32[352,128]{1,0:T(8,128)S(1)} collective-permute-done((f32[352,128]{1,0:T(8,128)S(1)}, f32[352,128]{1,0:T(8,128)S(1)}, u32[]{:S(2)}, u32[]{:S(2)}) %collective-permute-start.4) | collective-permute-done | bytes 180256 | tf_op jit(solution)/shard_map/ppermute | solution.py:487
  31.6 0.0 collective-permute-done.5.refs_3_
  31.6 1.9 %shard_map.71.refs_0_.refs_3_ = f32[960,128]{1,0:T(8,128)S(1)} custom-call(s32[1]{0:T(128)} %bitcast.refs_0_, f32[576,128]{1,0:T(8,128)S(1)} %get-tuple-element.55.refs_1_.refs_11_.refs_2_, f32[352,128]{1,0:T(8,128)S(1)} %collective-permute-done.4.refs_2_, f32[352,128]{1,0:T(8,128)S(1)} %collective-permute-done.5.refs_3_, ...), custom_call_target="tpu_custom_call" | custom-call | tf_op jit(solution)/shard_map/pallas_call | solution.py:28
  33.5 0.0 copy-start
  33.6 1.0 %shard_map.72 = f32[16,1,128]{2,1,0:T(1,128)S(1)} custom-call(f32[960,128]{1,0:T(8,128)S(1)} %shard_map.71.refs_0_.refs_3_, f32[16,128,128]{2,1,0:T(8,128)S(1)} %get-tuple-element.47.refs_6_.refs_4_.refs_1_, f32[16,128,128]{2,1,0:T(8,128)S(1)} %get-tuple-element.48.refs_7_.refs_5_.refs_2_, f32[16,24,128]{2,1,0:T(8,128)S(1)} %get-tuple-element.42.refs_6_.refs_8_.refs_3_, ...), custom_call_target="tpu_custom_call" | custom-call | tf_op jit(solution)/shard_map/pallas_call | solution.py:28
  34.6 16.4 %all_to_all.10 = f32[16,1,128]{2,1,0:T(1,128)S(1)} all-to-all(f32[16,1,128]{2,1,0:T(1,128)S(1)} %shard_map.72), channel_id=1, replica_groups=mesh['gx'=32,'gy'=16] {'gy'}, dimensions={0} | all-to-all | bytes 16384 | tf_op jit(solution)/shard_map/all_to_all | solution.py:561
  51.0 24.7 %all_to_all.11.refs_0_ = f32[32,1,128]{2,1,0:T(1,128)S(1)} all-to-all(f32[32,1,128]{2,1,0:T(1,128)S(1)} %broadcast_in_dim.2), channel_id=1, replica_groups=mesh['gx'=32,'gy'=16] {'gx'}, dimensions={0} | all-to-all | bytes 32768 | tf_op jit(solution)/shard_map/all_to_all | solution.py:562
  75.7 0.9 %shard_map.73 = f32[19,2,8,128]{3,2,1,0:T(8,128)} custom-call(f32[32,1,128]{2,1,0:T(1,128)S(1)} %all_to_all.11.refs_0_, f32[19,2,8,128]{3,2,1,0:T(8,128)S(1)} %copy-done, f32[576,128]{1,0:T(8,128)S(1)} %get-tuple-element.55.refs_1_.refs_11_.refs_2_, f32[960,128]{1,0:T(8,128)S(1)} %shard_map.71.refs_0_.refs_3_), custom_call_target="tpu_custom_call" | custom-call | tf_op jit(solution)/shard_map/pallas_call | solution.py:28
  (4 shorter events, 0.1 us)
Async XLA Ops:
  1.1 11.7 %collective-permute-start = (f32[240,128]{1,0:T(8,128)S(1)}, f32[240,128]{1,0:T(8,128)S(1)}, u32[]{:S(2)}, u32[]{:S(2)}) collective-permute-start(f32[240,128]{1,0:T(8,128)S(1)} %get-tuple-element.35), channel_id=1, source_target_pairs={{0,1},{1,0},{2,3},{3,2},{4,5},{5,4},{6,7},{7,6},{8,9},{9,8},{10,11... | collective-permute-start | bytes 368648 | tf_op jit(solution)/shard_map/ppermute | solution.py:487
  9.9 6.2 %collective-permute-start.1 = (f32[240,128]{1,0:T(8,128)S(1)}, f32[240,128]{1,0:T(8,128)S(1)}, u32[]{:S(2)}, u32[]{:S(2)}) collective-permute-start(f32[240,128]{1,0:T(8,128)S(1)} %get-tuple-element.36), channel_id=1, source_target_pairs={{1,2},{2,1},{3,4},{4,3},{5,6},{6,5},{7,8},{8,7},{9,10},{10,9},{11,... | collective-permute-start | bytes 368648 | tf_op jit(solution)/shard_map/ppermute | solution.py:486
  16.1 6.1 %collective-permute-start.2 = (f32[320,128]{1,0:T(8,128)S(1)}, f32[320,128]{1,0:T(8,128)S(1)}, u32[]{:S(2)}, u32[]{:S(2)}) collective-permute-start(f32[320,128]{1,0:T(8,128)S(1)} %get-tuple-element.45), channel_id=1, source_target_pairs={{0,16},{16,0},{32,48},{48,32},{64,80},{80,64},{96,112},{112,96},{1... | collective-permute-start | bytes 491528 | tf_op jit(solution)/shard_map/ppermute | solution.py:487
  18.0 4.1 %collective-permute-start.3 = (f32[320,128]{1,0:T(8,128)S(1)}, f32[320,128]{1,0:T(8,128)S(1)}, u32[]{:S(2)}, u32[]{:S(2)}) collective-permute-start(f32[320,128]{1,0:T(8,128)S(1)} %get-tuple-element.46), channel_id=1, source_target_pairs={{16,32},{32,16},{48,64},{64,48},{80,96},{96,80},{112,128},{128,112... | collective-permute-start | bytes 491528 | tf_op jit(solution)/shard_map/ppermute | solution.py:486
  23.5 8.2 %collective-permute-start.4 = (f32[352,128]{1,0:T(8,128)S(1)}, f32[352,128]{1,0:T(8,128)S(1)}, u32[]{:S(2)}, u32[]{:S(2)}) collective-permute-start(f32[352,128]{1,0:T(8,128)S(1)} %get-tuple-element.56), channel_id=1, source_target_pairs={{0,16},{16,0},{32,48},{48,32},{64,80},{80,64},{96,112},{112,96},{1... | collective-permute-start | bytes 540680 | tf_op jit(solution)/shard_map/ppermute | solution.py:487
  28.7 2.9 %collective-permute-start.5 = (f32[352,128]{1,0:T(8,128)S(1)}, f32[352,128]{1,0:T(8,128)S(1)}, u32[]{:S(2)}, u32[]{:S(2)}) collective-permute-start(f32[352,128]{1,0:T(8,128)S(1)} %get-tuple-element.57), channel_id=1, source_target_pairs={{16,32},{32,16},{48,64},{64,48},{80,96},{96,80},{112,128},{128,112... | collective-permute-start | bytes 540680 | tf_op jit(solution)/shard_map/ppermute | solution.py:486
  33.5 42.2 %copy-start = (f32[19,2,8,128]{3,2,1,0:T(8,128)S(1)}, f32[19,2,8,128]{3,2,1,0:T(8,128)}, u32[]{:S(2)}) copy-start(f32[19,2,8,128]{3,2,1,0:T(8,128)} %refs_1_.3) | copy-start | bytes 466948

commit v3 on v2

--- a/solution.py
+++ b/solution.py
@@ -351,15 +351,16 @@
         image[pl.ds((x * height + row + 2) * ROWS, ROWS), :] = value
 
     near = height * ROWS
-    face_tail(near, height, to_first, to_second)
     apply_rows(range(sx), -2, sy + 2, get, table_of(sx, sy, tables), weights, put, SPANS[0])
     odd = odd_x[0] == 1
     columns = offset_by(odd, 0, (sx - 1) * near)
     faces = offset_by(odd, near, (sx - 2) * near + 8)
     for out, at, face_at in zip((to_first, to_second), columns, faces):
-        out[pl.ds(0, near), :] = image[pl.ds(at, near), :]
         for row in range(height):
-            face(out, near, row, image[pl.ds(face_at + row * ROWS, 8), :])
+            here = row * ROWS
+            out[pl.ds(here, 16), :] = image[pl.ds(at + here, 16), :]
+            crossing = pltpu.roll(image[pl.ds(face_at + here, 8), :], Q - 16, 0)
+            out[pl.ds(here + 16, 8), :] = jnp.where(sublane() < Q - 16, image[pl.ds(at + here + 16, 8), :], crossing)
 
 
 def second_kernel(sx, sy, odd_x, previous, first, second, *refs):
@@ -372,7 +373,7 @@
             return previous[pl.ds((x * height + row + 2) * ROWS + group, 8), :]
         if x in (-1, sx):
             return beside((row + 2) * ROWS + group)[0 if x < 0 else 1]
-        return beside(height * ROWS + (row + 2) * FACE)[0 if x < 0 else 1]
+        return pltpu.roll(beside((row + 2) * ROWS + 16)[0 if x < 0 else 1], 24 - Q, 0)
 
     def put(x, row, value):
         image[pl.ds(((x + 1) * (sy + 2) + row + 1) * ROWS, ROWS), :] = value
@@ -535,7 +536,7 @@
     )
     tables_here, weights = (*own_table, *halo_table), (leave_rows, middle_t_wide, enter_t_wide)
     height = sy + 4
-    side_message = (height * ROWS + face_rows(height), sz)
+    side_message = (height * ROWS, sz)
     image_one, to_first, to_second = call(
         bind(first_kernel, sx, sy),
         [((sx * height * ROWS, sz), F32), (side_message, F32), (side_message, F32)],

time: 77 us -> 76.6 us (level)
  no operation moved by 1% of the time
where the time goes in v3:
time: 76.6 us; the launch traced here: 76.3 us
  blocking collectives  41.1 us (54%)
  starting transfers between devices  19.2 us (25%)
  Pallas kernels  8.85 us (12%)
  waiting for transfers between devices  6.93 us (9%)
    all_to_all x1, blocking collectives, per_device(): parts = lax.all_to_all(jnp.broadcast_to(line, (count_x, 1, sz)), 'gx', 0, 0)  25 us
    all_to_all x1, blocking collectives, per_device(): line = jnp.sum(lax.all_to_all(line, 'gy', 0, 0), axis=0, keepdims=True)  16.1 us
    ppermute x3, starting transfers between devices, exchange(): first = lax.ppermute(to_first, axis, near)  16 us
    pallas_call x9, Pallas kernels, call(): pl.pallas_call(kernel, out_shape=[jax.ShapeDtypeStruct(shape, kind) for s...  7.76 us
    ppermute x3, waiting for transfers between devices, exchange(): first = lax.ppermute(to_first, axis, near)  3.66 us
    ppermute x3, waiting for transfers between devices, exchange(): second = lax.ppermute(to_second, axis, far)  3.27 us
    ppermute x3, starting transfers between devices, exchange(): second = lax.ppermute(to_second, axis, far)  3.26 us
  transfers between devices with their start and end apart: 6, of which 3 were waited for; matrix products, arithmetic and copies ran while one was open for 0% of the time, Pallas kernels for 3%

profile of v3, /device:TPU:1, one launch (start us, length us, event | category | flops | bytes accessed | tf_op | source)
XLA Modules:
  0.0 76.3 jit_solution(7322874676297094357)
XLA Ops:
  0.0 1.1 %shard_map.64 = (f32[384,128]{1,0:T(8,128)S(1)}, f32[384,128]{1,0:T(8,128)S(1)}, f32[240,128]{1,0:T(8,128)S(1)}, f32[240,128]{1,0:T(8,128)S(1)}, f32[19,128]{1,0...) custom-call(f32[19,2,8,128]{3,2,1,0:T(8,128)} %refs_1_.3, f32[19,2,8,128]{3,2,1,0:T(8,128)} %refs_1_.2, ...), custom_call_target="tpu_custom_call" | custom-call | tf_op jit(solution)/shard_map/pallas_call | solution.py:507
  1.1 8.7 %collective-permute-start = (f32[240,128]{1,0:T(8,128)S(1)}, f32[240,128]{1,0:T(8,128)S(1)}, u32[]{:S(2)}, u32[]{:S(2)}) collective-permute-start(f32[240,128]{1,0:T(8,128)S(1)} %get-tuple-element.35), channel_id=1, source_target_pairs={{0,1},{1,0},{2,3},{3,2},{4,5},{5,4},{6,7},{7,6},{8,9},{9,8},{10,11... | collective-permute-start | bytes 368648 | tf_op jit(solution)/shard_map/ppermute | solution.py:488
  9.9 1.9 %collective-permute-start.1 = (f32[240,128]{1,0:T(8,128)S(1)}, f32[240,128]{1,0:T(8,128)S(1)}, u32[]{:S(2)}, u32[]{:S(2)}) collective-permute-start(f32[240,128]{1,0:T(8,128)S(1)} %get-tuple-element.36), channel_id=1, source_target_pairs={{1,2},{2,1},{3,4},{4,3},{5,6},{6,5},{7,8},{8,7},{9,10},{10,9},{11,... | collective-permute-start | bytes 368648 | tf_op jit(solution)/shard_map/ppermute | solution.py:487
  11.8 0.1 shard_map.65
  11.9 0.8 %shard_map.66 = (f32[16,128,128]{2,1,0:T(8,128)S(1)}, f32[16,128,128]{2,1,0:T(8,128)S(1)}, f32[16,24,128]{2,1,0:T(8,128)S(1)}) custom-call(f32[384,128]{1,0:T(8,128)S(1)} %get-tuple-element.34.refs_0_.refs_3_, bf16[128,128]{1,0:T(8,128)(2,1)S(1)} %get-tuple-element.40.refs_1_.refs_2_.refs_3_, bf16[256,256]{1,0:T(8,128)(2,1)S(1)} %get-tuple-element.41.refs_2_.refs_3_.refs_4_), custom_call_target="tpu_custom_call" | custom-call | tf_op jit(solution)/shard_map/pallas_call | solution.py:28
  12.8 0.0 collective-permute-done.refs_4_
  12.8 3.3 %collective-permute-done.1.refs_5_ = f32[240,128]{1,0:T(8,128)S(1)} collective-permute-done((f32[240,128]{1,0:T(8,128)S(1)}, f32[240,128]{1,0:T(8,128)S(1)}, u32[]{:S(2)}, u32[]{:S(2)}) %collective-permute-start.1) | collective-permute-done | bytes 122912 | tf_op jit(solution)/shard_map/ppermute | solution.py:487
  16.1 1.9 %collective-permute-start.2 = (f32[320,128]{1,0:T(8,128)S(1)}, f32[320,128]{1,0:T(8,128)S(1)}, u32[]{:S(2)}, u32[]{:S(2)}) collective-permute-start(f32[320,128]{1,0:T(8,128)S(1)} %get-tuple-element.45), channel_id=1, source_target_pairs={{0,16},{16,0},{32,48},{48,32},{64,80},{80,64},{96,112},{112,96},{1... | collective-permute-start | bytes 491528 | tf_op jit(solution)/shard_map/ppermute | solution.py:488
  18.0 0.7 collective-permute-start.3
  18.7 0.5 shard_map.68
  19.2 2.9 %collective-permute-done.2.refs_4_.refs_1_ = f32[320,128]{1,0:T(8,128)S(1)} collective-permute-done((f32[320,128]{1,0:T(8,128)S(1)}, f32[320,128]{1,0:T(8,128)S(1)}, u32[]{:S(2)}, u32[]{:S(2)}) %collective-permute-start.2) | collective-permute-done | bytes 163872 | tf_op jit(solution)/shard_map/ppermute | solution.py:488
  22.2 0.0 collective-permute-done.3.refs_5_.refs_2_
  22.2 1.3 %shard_map.69 = (f32[576,128]{1,0:T(8,128)S(1)}, f32[288,128]{1,0:T(8,128)S(1)}, f32[288,128]{1,0:T(8,128)S(1)}) custom-call(s32[1]{0:T(128)} %bitcast.refs_0_, f32[384,128]{1,0:T(8,128)S(1)} %get-tuple-element.33.refs_2_.refs_1_.refs_10_, f32[240,128]{1,0:T(8,128)S(1)} %get-tuple-element.43.refs_0_.refs_2_, ...), custom_call_target="tpu_custom_call" | custom-call | tf_op jit(solution)/shard_map/pallas_call | solution.py:28
  23.5 5.3 %collective-permute-start.4 = (f32[288,128]{1,0:T(8,128)S(1)}, f32[288,128]{1,0:T(8,128)S(1)}, u32[]{:S(2)}, u32[]{:S(2)}) collective-permute-start(f32[288,128]{1,0:T(8,128)S(1)} %get-tuple-element.56), channel_id=1, source_target_pairs={{0,16},{16,0},{32,48},{48,32},{64,80},{80,64},{96,112},{112,96},{1... | collective-permute-start | bytes 442376 | tf_op jit(solution)/shard_map/ppermute | solution.py:488
  28.8 0.7 collective-permute-start.5
  29.4 1.1 %shard_map.70 = (f32[20,128,128]{2,1,0:T(8,128)S(1)}, f32[20,128,128]{2,1,0:T(8,128)S(1)}, f32[20,24,128]{2,1,0:T(8,128)S(1)}) custom-call(s32[1]{0:T(128)} %bitcast.refs_0_, f32[320,128]{1,0:T(8,128)S(1)} %collective-permute-done.2.refs_4_.refs_1_, f32[320,128]{1,0:T(8,128)S(1)} %collective-permute-done.3.refs_5_.refs_2_, ...), custom_call_target="tpu_custom_call" | custom-call | tf_op jit(solution)/shard_map/pallas_call | solution.py:28
  30.5 0.7 collective-permute-done.4.refs_2_
  31.3 0.0 collective-permute-done.5.refs_3_
  31.3 1.9 %shard_map.71.refs_0_.refs_3_ = f32[960,128]{1,0:T(8,128)S(1)} custom-call(s32[1]{0:T(128)} %bitcast.refs_0_, f32[576,128]{1,0:T(8,128)S(1)} %get-tuple-element.55.refs_1_.refs_11_.refs_2_, f32[288,128]{1,0:T(8,128)S(1)} %collective-permute-done.4.refs_2_, f32[288,128]{1,0:T(8,128)S(1)} %collective-permute-done.5.refs_3_, ...), custom_call_target="tpu_custom_call" | custom-call | tf_op jit(solution)/shard_map/pallas_call | solution.py:28
  33.2 0.0 copy-start
  33.2 1.0 %shard_map.72 = f32[16,1,128]{2,1,0:T(1,128)S(1)} custom-call(f32[960,128]{1,0:T(8,128)S(1)} %shard_map.71.refs_0_.refs_3_, f32[16,128,128]{2,1,0:T(8,128)S(1)} %get-tuple-element.47.refs_6_.refs_4_.refs_1_, f32[16,128,128]{2,1,0:T(8,128)S(1)} %get-tuple-element.48.refs_7_.refs_5_.refs_2_, f32[16,24,128]{2,1,0:T(8,128)S(1)} %get-tuple-element.42.refs_6_.refs_8_.refs_3_, ...), custom_call_target="tpu_custom_call" | custom-call | tf_op jit(solution)/shard_map/pallas_call | solution.py:28
  34.2 16.1 %all_to_all.10 = f32[16,1,128]{2,1,0:T(1,128)S(1)} all-to-all(f32[16,1,128]{2,1,0:T(1,128)S(1)} %shard_map.72), channel_id=1, replica_groups=mesh['gx'=32,'gy'=16] {'gy'}, dimensions={0} | all-to-all | bytes 16384 | tf_op jit(solution)/shard_map/all_to_all | solution.py:562
  50.3 25.0 %all_to_all.11.refs_0_ = f32[32,1,128]{2,1,0:T(1,128)S(1)} all-to-all(f32[32,1,128]{2,1,0:T(1,128)S(1)} %broadcast_in_dim.2), channel_id=1, replica_groups=mesh['gx'=32,'gy'=16] {'gx'}, dimensions={0} | all-to-all | bytes 32768 | tf_op jit(solution)/shard_map/all_to_all | solution.py:563
  75.3 0.9 %shard_map.73 = f32[19,2,8,128]{3,2,1,0:T(8,128)} custom-call(f32[32,1,128]{2,1,0:T(1,128)S(1)} %all_to_all.11.refs_0_, f32[19,2,8,128]{3,2,1,0:T(8,128)S(1)} %copy-done, f32[576,128]{1,0:T(8,128)S(1)} %get-tuple-element.55.refs_1_.refs_11_.refs_2_, f32[960,128]{1,0:T(8,128)S(1)} %shard_map.71.refs_0_.refs_3_), custom_call_target="tpu_custom_call" | custom-call | tf_op jit(solution)/shard_map/pallas_call | solution.py:28
  (4 shorter events, 0.1 us)
Async XLA Ops:
  1.1 11.7 %collective-permute-start = (f32[240,128]{1,0:T(8,128)S(1)}, f32[240,128]{1,0:T(8,128)S(1)}, u32[]{:S(2)}, u32[]{:S(2)}) collective-permute-start(f32[240,128]{1,0:T(8,128)S(1)} %get-tuple-element.35), channel_id=1, source_target_pairs={{0,1},{1,0},{2,3},{3,2},{4,5},{5,4},{6,7},{7,6},{8,9},{9,8},{10,11... | collective-permute-start | bytes 368648 | tf_op jit(solution)/shard_map/ppermute | solution.py:488
  9.9 6.2 %collective-permute-start.1 = (f32[240,128]{1,0:T(8,128)S(1)}, f32[240,128]{1,0:T(8,128)S(1)}, u32[]{:S(2)}, u32[]{:S(2)}) collective-permute-start(f32[240,128]{1,0:T(8,128)S(1)} %get-tuple-element.36), channel_id=1, source_target_pairs={{1,2},{2,1},{3,4},{4,3},{5,6},{6,5},{7,8},{8,7},{9,10},{10,9},{11,... | collective-permute-start | bytes 368648 | tf_op jit(solution)/shard_map/ppermute | solution.py:487
  16.1 6.1 %collective-permute-start.2 = (f32[320,128]{1,0:T(8,128)S(1)}, f32[320,128]{1,0:T(8,128)S(1)}, u32[]{:S(2)}, u32[]{:S(2)}) collective-permute-start(f32[320,128]{1,0:T(8,128)S(1)} %get-tuple-element.45), channel_id=1, source_target_pairs={{0,16},{16,0},{32,48},{48,32},{64,80},{80,64},{96,112},{112,96},{1... | collective-permute-start | bytes 491528 | tf_op jit(solution)/shard_map/ppermute | solution.py:488
  18.0 4.1 %collective-permute-start.3 = (f32[320,128]{1,0:T(8,128)S(1)}, f32[320,128]{1,0:T(8,128)S(1)}, u32[]{:S(2)}, u32[]{:S(2)}) collective-permute-start(f32[320,128]{1,0:T(8,128)S(1)} %get-tuple-element.46), channel_id=1, source_target_pairs={{16,32},{32,16},{48,64},{64,48},{80,96},{96,80},{112,128},{128,112... | collective-permute-start | bytes 491528 | tf_op jit(solution)/shard_map/ppermute | solution.py:487
  23.5 7.8 %collective-permute-start.4 = (f32[288,128]{1,0:T(8,128)S(1)}, f32[288,128]{1,0:T(8,128)S(1)}, u32[]{:S(2)}, u32[]{:S(2)}) collective-permute-start(f32[288,128]{1,0:T(8,128)S(1)} %get-tuple-element.56), channel_id=1, source_target_pairs={{0,16},{16,0},{32,48},{48,32},{64,80},{80,64},{96,112},{112,96},{1... | collective-permute-start | bytes 442376 | tf_op jit(solution)/shard_map/ppermute | solution.py:488
  28.8 2.5 %collective-permute-start.5 = (f32[288,128]{1,0:T(8,128)S(1)}, f32[288,128]{1,0:T(8,128)S(1)}, u32[]{:S(2)}, u32[]{:S(2)}) collective-permute-start(f32[288,128]{1,0:T(8,128)S(1)} %get-tuple-element.57), channel_id=1, source_target_pairs={{16,32},{32,16},{48,64},{64,48},{80,96},{96,80},{112,128},{128,112... | collective-permute-start | bytes 442376 | tf_op jit(solution)/shard_map/ppermute | solution.py:487
  33.2 42.1 %copy-start = (f32[19,2,8,128]{3,2,1,0:T(8,128)S(1)}, f32[19,2,8,128]{3,2,1,0:T(8,128)}, u32[]{:S(2)}) copy-start(f32[19,2,8,128]{3,2,1,0:T(8,128)} %refs_1_.3) | copy-start | bytes 466948
